TPU v7x, 256 devices: a whole 4x4x8 slice. The times are simulated.
256 devices in a mesh: ctx: 16 (over y, x), grp: 16 (over z, core).
Axes of the slice: x: 4, y: 4, z: 8, core: 2. Of those that a mesh axis runs over, the one named last changes fastest.
Arguments:
- q_in: bfloat16 [2048, 8192], P('ctx', 'grp'), may hold values from -170 to 170
- k_in: bfloat16 [2048, 8192], P('ctx', 'grp'), may hold values from -6 to 6
- v_in: bfloat16 [2048, 8192], P('ctx', 'grp'), may hold values from -6 to 6
- fir: float32 [3, 3, 8192], P(None, None, 'grp'), may hold values from -3 to 3
- skip: float32 [8192], P('grp'), may hold values from 0.2 to 1
- taps: bfloat16 [64, 2048], P('grp'), may hold values from -0.25 to 0.25
- segments: int32 [2048], P('ctx'), may hold values from 0 to 1, never falling along the last dimension, each value on 1 to 1920 neighbouring positions
- gain: float32 [8192], P('grp'), may hold values from 0.1 to 1.9
Outputs:
- mixed: bfloat16 [2048, 8192], P('ctx', 'grp')
All inputs are finite; a program needn't handle non-finite values.
Results may differ from a plain program's by a relative error of at most 0.0085.
Values may be sent and summed in bfloat16 or wider, within the bound.
No kernel may reach another device: no remote copies, remote signals or barrier semaphores. Data moves between devices by JAX's collectives and lax.ppermute only.
A program may use at most 64 MiB of HBM per device.

v0:
```python
import jax
import jax.numpy as jnp
from jax import lax
from jax.sharding import PartitionSpec as P

D = 8192
GW = 128


def shifted(value, axis, by):
    peers = lax.axis_size(axis)
    pairs = [(i, i + by) for i in range(peers) if 0 <= i + by < peers]
    return lax.ppermute(value, axis, pairs)


def band_rect(padded_taps, pad_left, lag_base, rows, cols):
    length = rows + cols - 1
    window = lax.dynamic_slice_in_dim(padded_taps, lag_base - cols + 1 + pad_left, length, 0)
    flipped = jnp.concatenate([window[::-1], jnp.zeros((1,), padded_taps.dtype)])
    tiled = jnp.tile(flipped, rows)[: rows * length].reshape(rows, length)
    return tiled[:, rows - 1 :]


def token_conv(product_kv, taps, all_segs, segments):
    rows_dev, width = product_kv.shape
    groups_local = width // GW
    total_rows = all_segs.shape[0]
    my_start = lax.axis_index("ctx") * rows_dev
    margin = jnp.zeros((total_rows,), taps.dtype)
    padded_taps = [jnp.concatenate([margin, taps[group], margin]) for group in range(groups_local)]
    empty = jnp.zeros((rows_dev, width), jnp.float32)
    piece = lax.all_gather(product_kv, "ctx", axis=0, tiled=True)
    count = piece.shape[0]
    needed = (jnp.int32(0) <= my_start + rows_dev - 1) & (all_segs[-1] >= segments[0])
    allowed = segments[:, None] == all_segs[None, :]

    def work(total):
        parts_out = []
        for group in range(groups_local):
            matrix = band_rect(padded_taps[group], total_rows, my_start, rows_dev, count)
            matrix = jnp.where(allowed, matrix, jnp.zeros((), matrix.dtype))
            parts_out.append(
                jnp.dot(
                    matrix,
                    piece[:, group * GW : (group + 1) * GW],
                    preferred_element_type=jnp.float32,
                )
            )
        return total + jnp.concatenate(parts_out, axis=1)

    return lax.cond(needed, work, lambda total: total, empty)


def on_device(q_in, k_in, v_in, fir, skip, taps, segments, gain):
    rows_dev, width = q_in.shape
    stacked = jnp.stack([q_in, k_in, v_in])
    before = shifted(stacked[:, rows_dev - 2 :, :], "ctx", 1)
    padded = jnp.concatenate([before, stacked], axis=1).astype(jnp.float32)
    filtered = (
        fir[:, 0, None, :] * padded[:, 2:]
        + fir[:, 1, None, :] * padded[:, 1:-1]
        + fir[:, 2, None, :] * padded[:, :-2]
    )
    product_kv = (filtered[1] * filtered[2]).astype(jnp.bfloat16)
    all_segs = lax.all_gather(segments, "ctx", axis=0, tiled=True)
    conv = token_conv(product_kv, taps, all_segs, segments)
    gated = filtered[0] * (conv + skip * product_kv.astype(jnp.float32))
    squares = lax.psum(jnp.sum(gated * gated, axis=1), "grp")
    mixed = gated * lax.rsqrt(squares[:, None] / D + 1e-06) * gain
    return mixed.astype(jnp.bfloat16)


def solution(mesh):
    return jax.shard_map(
        on_device,
        mesh=mesh,
        in_specs=(
            P("ctx", "grp"),
            P("ctx", "grp"),
            P("ctx", "grp"),
            P(None, None, "grp"),
            P("grp"),
            P("grp", None),
            P("ctx"),
            P("grp"),
        ),
        out_specs=P("ctx", "grp"),
        check_vma=False,
    )
```

profile of v0, /device:TPU:1, one launch (start us, length us, event | category | flops | bytes accessed | tf_op | source)
XLA Modules:
  0.0 115.0 jit_solution(7496650928341975166)
XLA Ops:
  6.5 0.0 all-gather.4.cloned.1.call-start
  6.5 0.7 pad_maximum_fusion.13
  7.3 3.9 %collective-permute-start = (bf16[3,2,512]{2,1,0:T(2,128)(2,1)S(1)}, bf16[3,2,512]{2,1,0:T(2,128)(2,1)S(1)}, u32[]{:S(2)}, u32[]{:S(2)}) collective-permute-start(bf16[3,2,512]{2,1,0:T(2,128)(2,1)S(1)} %pad_maximum_fusion.13), channel_id=1, source_target_pairs={{0,16},{16,32},{32,48},{48,64},{64,80},{80,96},{96,112},{112,128},... | collective-permute-start | bytes 18440 | tf_op jit(solution)/shard_map/ppermute | solution.py:13
  11.2 0.9 fusion.33
  12.1 0.0 collective-permute-done
  12.1 1.1 maximum_convert_fusion
  13.3 0.0 copy-start.3
  13.3 0.0 copy-start
  13.3 0.2 fusion.28
  13.6 0.7 fusion.30
  14.3 0.0 all-gather.4.cloned.1.call-update
  14.3 0.0 copy-done.3
  14.3 18.4 %all-gather.1 = s32[16,1,128]{2,1,0:T(1,128)S(1)} all-gather(s32[1,1,128]{2,1,0:T(1,128)S(1)} %bitcast.55), channel_id=1, replica_groups=mesh['ctx'=16,'grp'=16] {'ctx'}, dimensions={0}, use_global_device_ids=true | all-gather | bytes 8704 | tf_op jit(solution)/shard_map/all_gather | solution.py:65
  32.7 0.6 slice.112
  33.9 0.1 slice_reduce_fusion
  34.1 34.0 %all-gather.4.cloned.1.call-done = bf16[1,2048,512]{2,1,0:T(8,128)(2,1)} async-done(((bf16[1,128,512]{2,1,0:T(8,128)(2,1)}), bf16[1,2048,512]{2,1,0:T(8,128)(2,1)}) %all-gather.4.cloned.1.call-update) | async-done | bytes 2097168 | tf_op jit(solution)/shard_map/all_gather | solution.py:32
  68.0 14.3 %conditional.1 = (f32[128,512]{1,0:T(8,128)S(1)}) conditional(s32[]{:T(128)} %convert_element_type.19, () %tuple.11, (s32[128]{0:T(128)S(1)}, s32[2048]{0:T(1024)S(1)}, s32[]{:T(128)}, bf16[6144]{0:T(1024)(128)(2,1)S(1)}, bf16[2048,512]{1,0:T(8,128)(2,1)}, /*index=5*/bf16[6144]{0:T(1024)(128)(2,1)S(1)}, bf16[6144]{0:T(1024)(128)(2,1)S(1)}, ...), branch_computations={%region_0.0_spmd, %region_1.2_spmd} | conditional | flops 270759680 | bytes 16835618 | solution.py:51
  68.0 0.1 dynamic_slice.8
  68.1 0.1 reverse.3
  68.2 0.1 slice.168
  68.3 0.1 dynamic_slice.9
  68.4 0.1 reverse.2
  68.5 0.1 slice.167
  68.5 0.1 pad_maximum_fusion.3
  68.6 0.1 dynamic_slice.10
  68.7 0.1 dynamic_slice.11
  68.8 0.1 reverse
  68.9 0.1 slice.165
  69.0 0.1 reverse.1
  69.1 0.1 slice.166
  69.1 0.1 pad_maximum_fusion.1
  69.3 0.6 tile.7
  69.9 1.0 reshape.26
  70.9 1.6 %fusion.3 = f32[128,128]{0,1:T(8,128)S(1)} fusion(bf16[128,2175]{1,0:T(8,128)(2,1)S(1)} %reshape.26, bf16[2048,512]{1,0:T(8,128)(2,1)} %get-tuple-element.31, s32[2048]{0:T(1024)S(1)} %get-tuple-element.28, s32[128]{0:T(128)S(1)} %get-tuple-element.27), kind=kOutput, calls=%fused_computation.7 | convolution fusion | flops 67633152 | bytes 1122816 | tf_op jit(solution)/shard_map/cond/branch_1_fun/dot_general | solution.py:43
  72.5 0.6 tile.3
  73.1 1.0 reshape.24
  74.1 1.6 %fusion.1 = f32[128,128]{0,1:T(8,128)S(1)} fusion(bf16[128,2175]{1,0:T(8,128)(2,1)S(1)} %reshape.24, bf16[2048,512]{1,0:T(8,128)(2,1)} %get-tuple-element.31, s32[2048]{0:T(1024)S(1)} %get-tuple-element.28, s32[128]{0:T(128)S(1)} %get-tuple-element.27), kind=kOutput, calls=%fused_computation.5 | convolution fusion | flops 67633152 | bytes 1122816 | tf_op jit(solution)/shard_map/cond/branch_1_fun/dot_general | solution.py:43
  75.7 0.6 tile.5
  76.4 1.0 reshape.25
  77.3 1.6 %fusion.2 = f32[128,128]{0,1:T(8,128)S(1)} fusion(bf16[128,2175]{1,0:T(8,128)(2,1)S(1)} %reshape.25, bf16[2048,512]{1,0:T(8,128)(2,1)} %get-tuple-element.31, s32[2048]{0:T(1024)S(1)} %get-tuple-element.28, s32[128]{0:T(128)S(1)} %get-tuple-element.27), kind=kOutput, calls=%fused_computation.6 | convolution fusion | flops 67633152 | bytes 1122816 | tf_op jit(solution)/shard_map/cond/branch_1_fun/dot_general | solution.py:43
  79.0 0.6 tile.1
  79.6 1.0 reshape.23
  80.6 1.6 %fusion = f32[128,128]{0,1:T(8,128)S(1)} fusion(bf16[128,2175]{1,0:T(8,128)(2,1)S(1)} %reshape.23, bf16[2048,512]{1,0:T(8,128)(2,1)} %get-tuple-element.31, s32[2048]{0:T(1024)S(1)} %get-tuple-element.28, s32[128]{0:T(128)S(1)} %get-tuple-element.27), kind=kOutput, calls=%fused_computation.4 | convolution fusion | flops 67633152 | bytes 1122816 | tf_op jit(solution)/shard_map/cond/branch_1_fun/dot_general | solution.py:43
  82.2 0.1 copy.13
  82.3 0.0 copy-done.1
  82.3 0.2 multiply_reduce_fusion
  82.5 24.9 %psum.7 = f32[128]{0:T(128)S(1)} all-reduce(f32[128]{0:T(128)S(1)} %multiply_reduce_fusion), channel_id=1, replica_groups=mesh['ctx'=16,'grp'=16] {'grp'}, use_global_device_ids=true, to_apply=%region_3.4 | all-reduce | flops 128 | bytes 1024 | tf_op jit(solution)/shard_map/psum | solution.py:68
  107.3 0.8 multiply_convert_fusion
  (14 shorter events, 0.2 us)
Async XLA Ops:
  6.5 61.5 %all-gather.4.cloned.1.call-start = ((), (), s32[]{:S(2)}) async-start(), calls=%async_computation | async-start | bytes 2228224 | tf_op jit(solution)/shard_map/all_gather | solution.py:32
  7.3 4.9 %collective-permute-start = (bf16[3,2,512]{2,1,0:T(2,128)(2,1)S(1)}, bf16[3,2,512]{2,1,0:T(2,128)(2,1)S(1)}, u32[]{:S(2)}, u32[]{:S(2)}) collective-permute-start(bf16[3,2,512]{2,1,0:T(2,128)(2,1)S(1)} %pad_maximum_fusion.13), channel_id=1, source_target_pairs={{0,16},{16,32},{32,48},{48,64},{64,80},{80,96},{96,112},{112,128},... | collective-permute-start | bytes 18440 | tf_op jit(solution)/shard_map/ppermute | solution.py:13
  13.3 1.0 copy-start.3
  13.3 20.6 %copy-start = (bf16[4,2048]{1,0:T(4,128)(2,1)S(1)}, bf16[4,2048]{1,0:T(4,128)(2,1)}, u32[]{:S(2)}) copy-start(bf16[4,2048]{1,0:T(4,128)(2,1)} %param.15) | copy-start | bytes 49156
  68.0 14.3 %copy-start.1 = (f32[512]{0:T(512)S(1)}, f32[512]{0:T(512)}, u32[]{:S(2)}) copy-start(f32[512]{0:T(512)} %param.14) | copy-start | bytes 6148
  68.0 39.3 %copy-start.2 = (f32[512]{0:T(512)S(1)}, f32[512]{0:T(512)}, u32[]{:S(2)}) copy-start(f32[512]{0:T(512)} %param.17) | copy-start | bytes 6148
Sparse Core Ops, SparseCore 0:
  14.4 53.5 all-gather.3
where the time goes:
time: 116 us; the launch traced here: 115 us
  blocking collectives  43.3 us (37%)
  waiting for transfers between devices  34 us (29%)
  between operations  14.1 us (12%)
  local copies, waits for them, and re-layouts  9.3 us (8%)
  matrix products  6.32 us (5%)
  starting transfers between devices  3.95 us (3%)
  other arithmetic  3.92 us (3%)
    all_gather x1, waiting for transfers between devices, token_conv(): piece = lax.all_gather(product_kv, 'ctx', axis=0, tiled=True)  34 us
    psum x1, blocking collectives, on_device(): squares = lax.psum(jnp.sum(gated * gated, axis=1), 'grp')  24.9 us
    all_gather x1, blocking collectives, on_device(): all_segs = lax.all_gather(segments, 'ctx', axis=0, tiled=True)  18.4 us
    dot_general x4, matrix products, work(): jnp.dot(matrix, piece[:, group * GW:(group + 1) * GW], preferred_element_...  6.32 us
    ppermute x1, starting transfers between devices, shifted(): return lax.ppermute(value, axis, pairs)  3.94 us
    reshape x4, local copies, waits for them, and re-layouts, band_rect(): tiled = jnp.tile(flipped, rows)[:rows * length].reshape(rows, length)  3.87 us
    another operation x8, local copies, waits for them, and re-layouts, band_rect(): tiled = jnp.tile(flipped, rows)[:rows * length].reshape(rows, length)  2.64 us
  transfers between devices with their start and end apart: 2, of which 1 were waited for; matrix products, arithmetic and copies ran while one was open for 1% of the time, Pallas kernels for 0%

commit v1 on v0

v1 whole, which is shorter than its diff:
```python
import jax
import jax.numpy as jnp
from jax import lax
from jax.experimental import pallas as pl
from jax.experimental.pallas import tpu as pltpu
from jax.sharding import PartitionSpec as P

D = 8192
GW = 128
NB = 16
TB = 128
CH = 32
ROWS = 3 * CH + 16


def pack_kernel(q_ref, k_ref, v_ref, seg_ref, out_ref):
    for n, ref in enumerate((k_ref, v_ref, q_ref)):
        value = ref[...].astype(jnp.float32).T.astype(jnp.bfloat16)
        out_ref[:, n * CH : (n + 1) * CH, :] = value.reshape(NB, CH, TB)
    seg = seg_ref[...].astype(jnp.float32).astype(jnp.bfloat16)
    out_ref[:, 3 * CH :, :] = jnp.broadcast_to(seg.reshape(1, 1, TB), (NB, ROWS - 3 * CH, TB))


def conv_kernel(idx_ref, x_ref, fir_ref, skip_ref, taps_ref, out_ref, coef_ref):
    index = idx_ref[0]
    tile = pl.multiple_of((index // 4) * GW, GW)
    rows = [fir_ref[a, :, pl.ds(tile, GW)] for a in range(3)]
    rows.append(skip_ref[:, pl.ds(tile, GW)])
    rows.append(jnp.zeros((6, GW), jnp.float32))
    coef_ref[:, 0:16] = jnp.concatenate(rows, axis=0).T
    coef = coef_ref[pl.ds(pl.multiple_of((index % 4) * CH, CH), CH), :]
    weights = [jnp.broadcast_to(coef[:, n : n + 1], (CH, TB)) for n in range(10)]

    taps = taps_ref[...].astype(jnp.float32)
    pick = lax.broadcasted_iota(jnp.int32, taps.shape, 0) == index // 4
    row = jnp.sum(jnp.where(pick, taps, 0.0), axis=0, keepdims=True)
    row_at = lax.broadcasted_iota(jnp.int32, (TB, TB), 0)
    col_at = lax.broadcasted_iota(jnp.int32, (TB, TB), 1)
    upper = col_at >= row_at
    before = jnp.zeros((TB, TB), jnp.float32)
    band = [jnp.zeros((TB, TB), jnp.bfloat16)]
    for m in range(NB):
        rolled = pltpu.roll(
            jnp.broadcast_to(row[:, m * TB : (m + 1) * TB], (TB, TB)), 0, 1, stride=1, stride_axis=0
        )
        band.append(jnp.where(upper, rolled, before).astype(jnp.bfloat16))
        before = rolled

    lane = lax.broadcasted_iota(jnp.int32, (CH, TB), 1)

    def filtered(a, which):
        lo, w = which * CH, ((3, 4, 5), (6, 7, 8), (0, 1, 2))[which]
        here = x_ref[a, lo : lo + CH, :].astype(jnp.float32)
        past = x_ref[a - 1, lo : lo + CH, :].astype(jnp.float32) if a else jnp.zeros_like(here)
        one = jnp.where(lane >= 1, pltpu.roll(here, 1, 1), pltpu.roll(past, 1, 1))
        two = jnp.where(lane >= 2, pltpu.roll(here, 2, 1), pltpu.roll(past, 2, 1))
        return weights[w[0]] * here + weights[w[1]] * one + weights[w[2]] * two

    product, second = [], []
    for a in range(NB):
        value = (filtered(a, 0) * filtered(a, 1)).astype(jnp.bfloat16)
        product.append(value)
        mask = x_ref[a, 3 * CH : 3 * CH + 1, :]
        second.append(value * mask)
    pairs = NB // 2
    lhs = []
    for source in (product, second):
        for pair in range(pairs):
            lhs.append(jnp.concatenate([source[2 * pair], source[2 * pair + 1]], axis=1))
    total = [None] * (2 * pairs)
    for d in range(pairs):
        matrix = jnp.concatenate(
            [
                jnp.concatenate([band[2 * d + 1], band[2 * d + 2]], axis=1),
                jnp.concatenate([band[2 * d], band[2 * d + 1]], axis=1),
            ],
            axis=0,
        )
        used = lhs[: pairs - d] + lhs[pairs : 2 * pairs - d]
        result = jnp.dot(jnp.concatenate(used, axis=0), matrix, preferred_element_type=jnp.float32)
        for n in range(pairs - d):
            for half in range(2):
                piece = result[(half * (pairs - d) + n) * CH :][:CH]
                at = half * pairs + n + d
                total[at] = piece if total[at] is None else total[at] + piece
    for a in range(NB):
        side = slice((a % 2) * TB, (a % 2 + 1) * TB)
        mask = x_ref[a, 3 * CH : 3 * CH + 1, :].astype(jnp.float32)
        conv = jnp.where(mask > 0.5, total[pairs + a // 2][:, side], total[a // 2][:, side])
        gated = filtered(a, 2) * (conv + weights[9] * product[a].astype(jnp.float32))
        out_ref[a] = gated.astype(jnp.bfloat16)


def square_kernel(x_ref, out_ref):
    value = x_ref[...].astype(jnp.float32)
    out_ref[...] = jnp.broadcast_to(jnp.sum(value * value, axis=0, keepdims=True), (NB, 1, TB))


def finish_kernel(x_ref, part_ref, gain_ref, out_ref):
    squares = jnp.sum(part_ref[...], axis=0)
    scale = lax.rsqrt(squares / D + 1e-06)
    value = (x_ref[...].astype(jnp.float32) * scale).T
    out_ref[...] = (value * gain_ref[...]).astype(jnp.bfloat16)


def on_device(q_in, k_in, v_in, fir, skip, taps, segments, gain):
    width = q_in.shape[1]
    payload = pl.pallas_call(
        pack_kernel, out_shape=jax.ShapeDtypeStruct((NB, ROWS, TB), jnp.bfloat16), name="pack"
    )(q_in, k_in, v_in, segments.reshape(1, TB))
    payload = lax.all_to_all(payload, "ctx", 0, 0, tiled=True)
    index = lax.axis_index("ctx").reshape(1)
    gated = pl.pallas_call(
        conv_kernel,
        out_shape=jax.ShapeDtypeStruct((NB, CH, TB), jnp.bfloat16),
        in_specs=[pl.BlockSpec(memory_space=pltpu.SMEM)] + [pl.BlockSpec(memory_space=pltpu.VMEM)] * 4,
        scratch_shapes=[pltpu.VMEM((GW, GW), jnp.float32)],
        name="conv",
    )(index, payload, fir, skip.reshape(1, width), taps)
    gated = lax.all_to_all(gated, "ctx", 0, 0, tiled=True).reshape(width, TB)
    part = pl.pallas_call(
        square_kernel, out_shape=jax.ShapeDtypeStruct((NB, 1, TB), jnp.float32), name="squares"
    )(gated)
    part = lax.all_to_all(part, "grp", 0, 0, tiled=True)
    return pl.pallas_call(
        finish_kernel, out_shape=jax.ShapeDtypeStruct((TB, width), jnp.bfloat16), name="finish"
    )(gated, part, gain.reshape(1, width))


def solution(mesh):
    return jax.shard_map(
        on_device,
        mesh=mesh,
        in_specs=(
            P("ctx", "grp"),
            P("ctx", "grp"),
            P("ctx", "grp"),
            P(None, None, "grp"),
            P("grp"),
            P("grp", None),
            P("ctx"),
            P("grp"),
        ),
        out_specs=P("ctx", "grp"),
        check_vma=False,
    )
```

time: 116 us -> 56.2 us (0.48)
  waiting for transfers between devices: 34 us -> 9.87 us
  between operations: 14.1 us -> 0.02 us
  blocking collectives: 43.3 us -> 29.5 us
  local copies, waits for them, and re-layouts: 9.3 us -> 0.77 us
  Pallas kernels: 0 us -> 8 us
  matrix products: 6.32 us -> 0 us
  other arithmetic: 3.92 us -> 0 us
  starting transfers between devices: 3.95 us -> 7.58 us
    all_gather x1 -> x0, waiting for transfers between devices: 34 us -> none  [token_conv(): piece = lax.all_gather(product_kv, 'ctx', axis=0, tiled=True)]
    all_to_all x0 -> x2, blocking collectives: none -> 29.5 us  [the longest x1 18.5 us: on_device(): part = lax.all_to_all(part, 'grp', 0, 0, tiled=True)]
    psum x1 -> x0, blocking collectives: 24.9 us -> none  [on_device(): squares = lax.psum(jnp.sum(gated * gated, axis=1), 'grp')]
    all_gather x1 -> x0, blocking collectives: 18.4 us -> none  [on_device(): all_segs = lax.all_gather(segments, 'ctx', axis=0, tiled=True)]
    all_to_all x0 -> x1, waiting for transfers between devices: none -> 9.87 us  [on_device(): payload = lax.all_to_all(payload, 'ctx', 0, 0, tiled=True)]
    pallas_call x0 -> x4, Pallas kernels: none -> 8 us  [the longest x1 2.7 us: on_device(): pl.pallas_call(conv_kernel, out_shape=jax.ShapeDtypeStruct((NB, CH, TB),...]
    all_to_all x0 -> x1, starting transfers between devices: none -> 7.58 us  [on_device(): payload = lax.all_to_all(payload, 'ctx', 0, 0, tiled=True)]
    dot_general x4 -> x0, matrix products: 6.32 us -> none  [work(): jnp.dot(matrix, piece[:, group * GW:(group + 1) * GW], preferred_element_...]
  transfers between devices with their start and end apart: 2 -> 1, of which waited for: 1 -> 1; matrix products, arithmetic and copies ran while one was open for 1% -> 0% of each run, Pallas kernels for 0% -> 0%
where the time goes in v1:
time: 56.2 us; the launch traced here: 55.8 us
  blocking collectives  29.5 us (52%)
  waiting for transfers between devices  9.87 us (18%)
  Pallas kernels  8 us (14%)
  starting transfers between devices  7.58 us (13%)
  local copies, waits for them, and re-layouts  0.77 us (1%)
    all_to_all x1, blocking collectives, on_device(): part = lax.all_to_all(part, 'grp', 0, 0, tiled=True)  18.5 us
    all_to_all x1, blocking collectives, on_device(): gated = lax.all_to_all(gated, 'ctx', 0, 0, tiled=True).reshape(width, TB)  11 us
    all_to_all x1, waiting for transfers between devices, on_device(): payload = lax.all_to_all(payload, 'ctx', 0, 0, tiled=True)  9.87 us
    all_to_all x1, starting transfers between devices, on_device(): payload = lax.all_to_all(payload, 'ctx', 0, 0, tiled=True)  7.58 us
    pallas_call x1, Pallas kernels, on_device(): pl.pallas_call(conv_kernel, out_shape=jax.ShapeDtypeStruct((NB, CH, TB),...  2.7 us
    pallas_call x1, Pallas kernels, on_device(): pl.pallas_call(pack_kernel, out_shape=jax.ShapeDtypeStruct((NB, ROWS, TB)...  1.98 us
    pallas_call x1, Pallas kernels, on_device(): pl.pallas_call(finish_kernel, out_shape=jax.ShapeDtypeStruct((TB, width),...  1.74 us
    pallas_call x1, Pallas kernels, on_device(): pl.pallas_call(square_kernel, out_shape=jax.ShapeDtypeStruct((NB, 1, TB),...  1.58 us
  transfers between devices with their start and end apart: 1, of which 1 were waited for; matrix products, arithmetic and copies ran while one was open for 0% of the time, Pallas kernels for 0%

profile of v1, /device:TPU:1, one launch (start us, length us, event | category | flops | bytes accessed | tf_op | source)
XLA Modules:
  0.0 55.8 jit_solution(17927783294270958209)
XLA Ops:
  0.0 2.0 %pack.1 = bf16[16,112,128]{2,1,0:T(8,128)(2,1)} custom-call(bf16[128,512]{1,0:T(8,128)(2,1)} %q_ref.1, bf16[128,512]{1,0:T(8,128)(2,1)} %k_ref.1, bf16[128,512]{1,0:T(8,128)(2,1)} %v_ref.1, s32[1,128]{1,0:T(1,128)} %bitcast.9), custom_call_target="tpu_custom_call" | custom-call | tf_op jit(solution)/shard_map/pack/pallas_call | solution.py:108
  2.0 7.6 %all-to-all-start = ((bf16[16,112,128]{2,1,0:T(8,128)(2,1)}), bf16[16,112,128]{2,1,0:T(8,128)(2,1)S(1)}, u32[]{:S(2)}, u32[]{:S(2)}) async-start(bf16[16,112,128]{2,1,0:T(8,128)(2,1)} %pack.1), calls=%async_computation | async-start | bytes 917504 | tf_op jit(solution)/shard_map/all_to_all | solution.py:111
  9.6 9.9 %all-to-all-done.x_ref = bf16[16,112,128]{2,1,0:T(8,128)(2,1)S(1)} async-done(((bf16[16,112,128]{2,1,0:T(8,128)(2,1)}), bf16[16,112,128]{2,1,0:T(8,128)(2,1)S(1)}, u32[]{:S(2)}, u32[]{:S(2)}) %all-to-all-start) | async-done | bytes 458784 | tf_op jit(solution)/shard_map/all_to_all | solution.py:111
  19.4 0.0 copy-start
  19.5 0.8 %copy-done = bf16[16,112,128]{2,1,0:T(8,128)(2,1)} copy-done((bf16[16,112,128]{2,1,0:T(8,128)(2,1)}, bf16[16,112,128]{2,1,0:T(8,128)(2,1)S(1)}, u32[]{:S(2)}) %copy-start) | copy-done | bytes 458776
  20.2 2.7 %conv.1 = bf16[16,32,128]{2,1,0:T(8,128)(2,1)} custom-call(s32[1]{0:T(128)} %bitcast.idx_ref, bf16[16,112,128]{2,1,0:T(8,128)(2,1)} %copy-done, f32[3,3,512]{2,1,0:T(4,128)} %fir_ref.1, f32[1,512]{1,0:T(1,128)} %bitcast.7, bf16[4,2048]{1,0:T(4,128)(2,1)} %taps_ref.1), custom_call_target="tpu_custom_call" | custom-call | tf_op jit(solution)/shard_map/conv/pallas_call | solution.py:113
  22.9 11.0 %all_to_all.15 = bf16[16,32,128]{2,1,0:T(8,128)(2,1)} all-to-all(bf16[16,32,128]{2,1,0:T(8,128)(2,1)} %conv.1), channel_id=1, replica_groups=mesh['ctx'=16,'grp'=16] {'ctx'}, dimensions={0} | all-to-all | bytes 262144 | tf_op jit(solution)/shard_map/all_to_all | solution.py:120
  33.9 1.6 %squares.1 = f32[16,1,128]{2,1,0:T(1,128)} custom-call(bf16[512,128]{1,0:T(8,128)(2,1)} %bitcast.5), custom_call_target="tpu_custom_call" | custom-call | tf_op jit(solution)/shard_map/squares/pallas_call | solution.py:121
  35.5 18.5 %all_to_all.16.part_ref = f32[16,1,128]{2,1,0:T(1,128)} all-to-all(f32[16,1,128]{2,1,0:T(1,128)} %squares.1), channel_id=1, replica_groups=mesh['ctx'=16,'grp'=16] {'grp'}, dimensions={0} | all-to-all | bytes 16384 | tf_op jit(solution)/shard_map/all_to_all | solution.py:124
  54.0 1.7 %finish.1 = bf16[128,512]{1,0:T(8,128)(2,1)} custom-call(bf16[512,128]{1,0:T(8,128)(2,1)} %bitcast.6, f32[16,1,128]{2,1,0:T(1,128)} %all_to_all.16.part_ref, f32[1,512]{1,0:T(1,128)} %bitcast.8), custom_call_target="tpu_custom_call" | custom-call | tf_op jit(solution)/shard_map/finish/pallas_call | solution.py:125
Async XLA Ops:
  2.0 17.5 %all-to-all-start = ((bf16[16,112,128]{2,1,0:T(8,128)(2,1)}), bf16[16,112,128]{2,1,0:T(8,128)(2,1)S(1)}, u32[]{:S(2)}, u32[]{:S(2)}) async-start(bf16[16,112,128]{2,1,0:T(8,128)(2,1)} %pack.1), calls=%async_computation | async-start | bytes 917504 | tf_op jit(solution)/shard_map/all_to_all | solution.py:111
  19.4 0.8 %copy-start = (bf16[16,112,128]{2,1,0:T(8,128)(2,1)}, bf16[16,112,128]{2,1,0:T(8,128)(2,1)S(1)}, u32[]{:S(2)}) copy-start(bf16[16,112,128]{2,1,0:T(8,128)(2,1)S(1)} %all-to-all-done.x_ref) | copy-start | bytes 1376260

commit v2 on v1

v2 whole, which is shorter than its diff:
```python
import jax
import jax.numpy as jnp
from jax import lax
from jax.experimental import pallas as pl
from jax.experimental.pallas import tpu as pltpu
from jax.sharding import PartitionSpec as P

D = 8192
GW = 128
NB = 16
TB = 128
CH = 32
HALO = 2 * CH
SEG = HALO + 8
ROWS = HALO + 16
F32 = jnp.float32
BF16 = jnp.bfloat16


def pack_kernel(k_ref, v_ref, q_ref, seg_ref, out_ref):
    for n, ref in enumerate((k_ref, v_ref)):
        value = ref[...].astype(F32).T.astype(BF16)
        out_ref[:, n * CH : (n + 1) * CH, :] = value.reshape(NB, CH, TB)
    tail = q_ref[TB - 16 :, :].astype(F32)[14:16]
    pieces = [tail[:, n * TB : (n + 1) * TB] for n in range(4)]
    pieces.append(jnp.broadcast_to(seg_ref[...].astype(F32), (8, TB)))
    extra = jnp.concatenate(pieces, axis=0).astype(BF16)
    out_ref[:, HALO:, :] = jnp.broadcast_to(extra.reshape(1, ROWS - HALO, TB), (NB, ROWS - HALO, TB))


def band_kernel(idx_ref, fir_ref, skip_ref, taps_ref, band_ref, weight_ref, coef_ref):
    index = idx_ref[0]
    tile = pl.multiple_of((index // 4) * GW, GW)
    rows = [fir_ref[a, :, pl.ds(tile, GW)] for a in (1, 2)]
    rows.append(skip_ref[:, pl.ds(tile, GW)])
    rows.append(jnp.zeros((1, GW), F32))
    coef_ref[:, 0:8] = jnp.concatenate(rows, axis=0).T
    coef = coef_ref[pl.ds(pl.multiple_of((index % 4) * CH, CH), CH), :]
    for n in range(7):
        weight_ref[n] = jnp.broadcast_to(coef[:, n : n + 1], (CH, TB))

    taps = taps_ref[...].astype(F32)
    pick = lax.broadcasted_iota(jnp.int32, taps.shape, 0) == index // 4
    row = jnp.sum(jnp.where(pick, taps, 0.0), axis=0, keepdims=True)
    row_at = lax.broadcasted_iota(jnp.int32, (TB, TB), 0)
    col_at = lax.broadcasted_iota(jnp.int32, (TB, TB), 1)
    upper = col_at >= row_at
    before = jnp.zeros((TB, TB), F32)
    band_ref[0] = before.astype(BF16)
    for m in range(NB):
        piece = jnp.broadcast_to(row[:, m * TB : (m + 1) * TB], (TB, TB))
        rolled = pltpu.roll(piece, 0, 1, stride=1, stride_axis=0)
        band_ref[m + 1] = jnp.where(upper, rolled, before).astype(BF16)
        before = rolled


def conv_kernel(x_ref, band_ref, weight_ref, out_ref):
    lane = lax.broadcasted_iota(jnp.int32, (CH, TB), 1)
    weights = [weight_ref[n] for n in range(7)]

    def filtered(a, which):
        lo = which * CH
        here = x_ref[a, lo : lo + CH, :].astype(F32)
        past = x_ref[a - 1, lo : lo + CH, :].astype(F32) if a else jnp.zeros_like(here)
        one = jnp.where(lane >= 1, pltpu.roll(here, 1, 1), pltpu.roll(past, 1, 1))
        two = jnp.where(lane >= 2, pltpu.roll(here, 2, 1), pltpu.roll(past, 2, 1))
        return weights[3 * which] * here + weights[3 * which + 1] * one + weights[3 * which + 2] * two

    product, second = [], []
    for a in range(NB):
        value = (filtered(a, 0) * filtered(a, 1)).astype(BF16)
        product.append(value)
        mask = x_ref[a, SEG : SEG + 1, :]
        second.append(value * mask)
    pairs = NB // 2
    lhs = []
    for source in (product, second):
        for pair in range(pairs):
            lhs.append(jnp.concatenate([source[2 * pair], source[2 * pair + 1]], axis=1))
    total = [None] * (2 * pairs)
    for d in range(pairs):
        matrix = jnp.concatenate(
            [
                jnp.concatenate([band_ref[2 * d + 1], band_ref[2 * d + 2]], axis=1),
                jnp.concatenate([band_ref[2 * d], band_ref[2 * d + 1]], axis=1),
            ],
            axis=0,
        )
        used = lhs[: pairs - d] + lhs[pairs : 2 * pairs - d]
        result = jnp.dot(jnp.concatenate(used, axis=0), matrix, preferred_element_type=F32)
        for n in range(pairs - d):
            for half in range(2):
                piece = result[(half * (pairs - d) + n) * CH :][:CH]
                at = half * pairs + n + d
                total[at] = piece if total[at] is None else total[at] + piece
    for a in range(NB):
        side = slice((a % 2) * TB, (a % 2 + 1) * TB)
        mask = x_ref[a, SEG : SEG + 1, :].astype(F32)
        conv = jnp.where(mask > 0.5, total[pairs + a // 2][:, side], total[a // 2][:, side])
        out_ref[a] = (conv + weights[6] * product[a].astype(F32)).astype(BF16)


def gate_kernel(idx_ref, q_ref, x_ref, fir_ref, out_ref):
    index = idx_ref[0]
    halo = x_ref[jnp.maximum(index - 1, 0)].astype(F32)[HALO : HALO + 8]
    halo = jnp.where(index > 0, halo, 0.0)
    row_at = lax.broadcasted_iota(jnp.int32, (TB, TB), 0)
    for n in range(4):
        lanes = slice(n * TB, (n + 1) * TB)
        here = q_ref[:, lanes].astype(F32)
        last, older = halo[2 * n + 1 : 2 * n + 2], halo[2 * n : 2 * n + 1]
        one = jnp.where(row_at == 0, last, pltpu.roll(here, 1, 0))
        two = jnp.where(row_at == 0, older, jnp.where(row_at == 1, last, pltpu.roll(here, 2, 0)))
        value = fir_ref[0, 0:1, lanes] * here + fir_ref[0, 1:2, lanes] * one + fir_ref[0, 2:3, lanes] * two
        out_ref[lanes, :] = value.T


def square_kernel(u_ref, gate_ref, out_ref):
    value = u_ref[...].astype(F32) * gate_ref[...]
    out_ref[...] = jnp.broadcast_to(jnp.sum(value * value, axis=0, keepdims=True), (NB, 1, TB))


def turn_kernel(u_ref, gate_ref, out_ref):
    for n in range(4):
        lanes = slice(n * TB, (n + 1) * TB)
        value = u_ref[lanes, :].astype(F32) * gate_ref[lanes, :]
        out_ref[:, lanes] = value.T


def finish_kernel(x_ref, part_ref, gain_ref, out_ref):
    squares = jnp.sum(part_ref[...], axis=0)
    scale = lax.rsqrt(squares / D + 1e-06)
    scale = jnp.broadcast_to(scale, (TB, TB)).T
    for n in range(4):
        lanes = slice(n * TB, (n + 1) * TB)
        out_ref[:, lanes] = (x_ref[:, lanes] * scale * gain_ref[:, lanes]).astype(BF16)


VM = pl.BlockSpec(memory_space=pltpu.VMEM)
SM = pl.BlockSpec(memory_space=pltpu.SMEM)


def keep(value):
    return pltpu.with_memory_space_constraint(value, pltpu.VMEM)


def on_device(q_in, k_in, v_in, fir, skip, taps, segments, gain):
    width = q_in.shape[1]
    index = lax.axis_index("ctx").reshape(1)
    payload = pl.pallas_call(
        pack_kernel,
        out_shape=pltpu.VMEM((NB, ROWS, TB), BF16),
        in_specs=[VM, VM, VM, VM],
        out_specs=VM,
        name="pack",
    )(k_in, v_in, q_in, segments.reshape(1, TB))
    payload = lax.all_to_all(payload, "ctx", 0, 0, tiled=True)
    band, weight = pl.pallas_call(
        band_kernel,
        out_shape=(pltpu.VMEM((NB + 1, TB, TB), BF16), pltpu.VMEM((7, CH, TB), F32)),
        in_specs=[SM, VM, VM, VM],
        out_specs=(VM, VM),
        scratch_shapes=[pltpu.VMEM((GW, GW), F32)],
        name="band",
    )(index, fir, skip.reshape(1, width), taps)
    mixed = pl.pallas_call(
        conv_kernel,
        out_shape=pltpu.VMEM((NB, CH, TB), BF16),
        in_specs=[VM, VM, VM],
        out_specs=VM,
        name="conv",
    )(keep(payload), keep(band), keep(weight))
    mixed = lax.all_to_all(mixed, "ctx", 0, 0, tiled=True).reshape(width, TB)
    gate = pl.pallas_call(
        gate_kernel,
        out_shape=pltpu.VMEM((width, TB), F32),
        in_specs=[SM, VM, VM, VM],
        out_specs=VM,
        name="gate",
    )(index, q_in, keep(payload), fir)
    part = pl.pallas_call(
        square_kernel,
        out_shape=pltpu.VMEM((NB, 1, TB), F32),
        in_specs=[VM, VM],
        out_specs=VM,
        name="squares",
    )(keep(mixed), keep(gate))
    part = lax.all_to_all(part, "grp", 0, 0, tiled=True)
    turned = pl.pallas_call(
        turn_kernel,
        out_shape=pltpu.VMEM((TB, width), F32),
        in_specs=[VM, VM],
        out_specs=VM,
        name="turn",
    )(keep(mixed), keep(gate))
    return pl.pallas_call(
        finish_kernel,
        out_shape=jax.ShapeDtypeStruct((TB, width), BF16),
        in_specs=[VM, VM, VM],
        out_specs=VM,
        name="finish",
    )(keep(turned), keep(part), gain.reshape(1, width))


def solution(mesh):
    return jax.shard_map(
        on_device,
        mesh=mesh,
        in_specs=(
            P("ctx", "grp"),
            P("ctx", "grp"),
            P("ctx", "grp"),
            P(None, None, "grp"),
            P("grp"),
            P("grp", None),
            P("ctx"),
            P("grp"),
        ),
        out_specs=P("ctx", "grp"),
        check_vma=False,
    )
```

time: 56.2 us -> 50.6 us (0.900)
  blocking collectives: 29.5 us -> 0 us
  starting transfers between devices: 7.58 us -> 22.6 us
  waiting for transfers between devices: 9.87 us -> 19.9 us
  local copies, waits for them, and re-layouts: 0.77 us -> 0 us
    all_to_all x2 -> x0, blocking collectives: 29.5 us -> none  [the longest x1 18.5 us: on_device(): part = lax.all_to_all(part, 'grp', 0, 0, tiled=True)]
    all_to_all x0 -> x2, starting transfers between devices: none -> 15 us  [the longest x1 11.5 us: on_device(): part = lax.all_to_all(part, 'grp', 0, 0, tiled=True)]
    all_to_all x0 -> x2, waiting for transfers between devices: none -> 12.5 us  [the longest x1 6.8 us: on_device(): part = lax.all_to_all(part, 'grp', 0, 0, tiled=True)]
    all_to_all x1, waiting for transfers between devices: 9.87 us -> 7.35 us  [on_device(): payload = lax.all_to_all(payload, 'ctx', 0, 0, tiled=True)]
    unnamed x2 -> x0, local copies, waits for them, and re-layouts: 0.77 us -> none
    pallas_call x3 -> x6, Pallas kernels: 6.26 us -> 6.19 us  [the longest x1 1.91 us: on_device(): pl.pallas_call(pack_kernel, out_shape=pltpu.VMEM((NB, ROWS, TB), BF16), i...]
  transfers between devices with their start and end apart: 1 -> 3, of which waited for: 1 -> 3; matrix products, arithmetic and copies ran while one was open for 0% -> 0% of each run, Pallas kernels for 0% -> 5%
where the time goes in v2:
time: 50.6 us; the launch traced here: 50.2 us
  starting transfers between devices  22.6 us (45%)
  waiting for transfers between devices  19.9 us (39%)
  Pallas kernels  7.66 us (15%)
    all_to_all x1, starting transfers between devices, on_device(): part = lax.all_to_all(part, 'grp', 0, 0, tiled=True)  11.5 us
    all_to_all x1, starting transfers between devices, on_device(): payload = lax.all_to_all(payload, 'ctx', 0, 0, tiled=True)  7.58 us
    all_to_all x1, waiting for transfers between devices, on_device(): payload = lax.all_to_all(payload, 'ctx', 0, 0, tiled=True)  7.35 us
    all_to_all x1, waiting for transfers between devices, on_device(): part = lax.all_to_all(part, 'grp', 0, 0, tiled=True)  6.8 us
    all_to_all x1, waiting for transfers between devices, on_device(): mixed = lax.all_to_all(mixed, 'ctx', 0, 0, tiled=True).reshape(width, TB)  5.73 us
    all_to_all x1, starting transfers between devices, on_device(): mixed = lax.all_to_all(mixed, 'ctx', 0, 0, tiled=True).reshape(width, TB)  3.51 us
    pallas_call x1, Pallas kernels, on_device(): pl.pallas_call(pack_kernel, out_shape=pltpu.VMEM((NB, ROWS, TB), BF16), i...  1.91 us
    pallas_call x1, Pallas kernels, on_device(): pl.pallas_call(finish_kernel, out_shape=jax.ShapeDtypeStruct((TB, width),...  1.47 us
  transfers between devices with their start and end apart: 3, of which 3 were waited for; matrix products, arithmetic and copies ran while one was open for 0% of the time, Pallas kernels for 5%

profile of v2, /device:TPU:1, one launch (start us, length us, event | category | flops | bytes accessed | tf_op | source)
XLA Modules:
  0.0 50.2 jit_solution(5589823894631197914)
XLA Ops:
  0.0 1.9 %pack.1 = bf16[16,80,128]{2,1,0:T(8,128)(2,1)} custom-call(bf16[128,512]{1,0:T(8,128)(2,1)} %k_ref.1, bf16[128,512]{1,0:T(8,128)(2,1)} %v_ref.1, bf16[128,512]{1,0:T(8,128)(2,1)} %q_ref.3, s32[1,128]{1,0:T(1,128)} %bitcast.9), custom_call_target="tpu_custom_call" | custom-call | tf_op jit(solution)/shard_map/pack/pallas_call | solution.py:150
  1.9 7.6 %all-to-all-start = ((bf16[16,80,128]{2,1,0:T(8,128)(2,1)}), bf16[16,80,128]{2,1,0:T(8,128)(2,1)S(1)}, u32[]{:S(2)}, u32[]{:S(2)}) async-start(bf16[16,80,128]{2,1,0:T(8,128)(2,1)} %pack.1), calls=%async_computation | async-start | bytes 655360 | tf_op jit(solution)/shard_map/all_to_all | solution.py:157
  9.5 1.1 %band.1 = (bf16[17,128,128]{2,1,0:T(8,128)(2,1)S(1)}, f32[7,32,128]{2,1,0:T(8,128)S(1)}) custom-call(s32[1]{0:T(128)} %bitcast.1.idx_ref, f32[3,3,512]{2,1,0:T(4,128)} %fir_ref.3, f32[1,512]{1,0:T(1,128)} %bitcast.8, bf16[4,2048]{1,0:T(4,128)(2,1)} %taps_ref.1), custom_call_target="tpu_custom_call" | custom-call | tf_op jit(solution)/shard_map/band/pallas_call | solution.py:158
  10.6 7.3 %all-to-all-done.x_ref = bf16[16,80,128]{2,1,0:T(8,128)(2,1)S(1)} async-done(((bf16[16,80,128]{2,1,0:T(8,128)(2,1)}), bf16[16,80,128]{2,1,0:T(8,128)(2,1)S(1)}, u32[]{:S(2)}, u32[]{:S(2)}) %all-to-all-start) | async-done | bytes 327712 | tf_op jit(solution)/shard_map/all_to_all | solution.py:157
  18.0 1.3 %conv.1 = bf16[16,32,128]{2,1,0:T(8,128)(2,1)} custom-call(bf16[16,80,128]{2,1,0:T(8,128)(2,1)S(1)} %all-to-all-done.x_ref, bf16[17,128,128]{2,1,0:T(8,128)(2,1)S(1)} %get-tuple-element.7.band_ref, f32[7,32,128]{2,1,0:T(8,128)S(1)} %get-tuple-element.8.weight_ref), custom_call_target="tpu_custom_call" | custom-call | tf_op jit(solution)/shard_map/conv/pallas_call | solution.py:166
  19.3 3.5 %all-to-all-start.1 = ((bf16[16,32,128]{2,1,0:T(8,128)(2,1)}), bf16[16,32,128]{2,1,0:T(8,128)(2,1)S(1)}, u32[]{:S(2)}, u32[]{:S(2)}) async-start(bf16[16,32,128]{2,1,0:T(8,128)(2,1)} %conv.1), calls=%async_computation.1 | async-start | bytes 262144 | tf_op jit(solution)/shard_map/all_to_all | solution.py:173
  22.8 1.1 %gate.1.gate_ref = f32[512,128]{1,0:T(8,128)S(1)} custom-call(s32[1]{0:T(128)} %bitcast.1.idx_ref, bf16[128,512]{1,0:T(8,128)(2,1)} %q_ref.3, bf16[16,80,128]{2,1,0:T(8,128)(2,1)S(1)} %all-to-all-done.x_ref, f32[3,3,512]{2,1,0:T(4,128)} %fir_ref.3), custom_call_target="tpu_custom_call" | custom-call | tf_op jit(solution)/shard_map/gate/pallas_call | solution.py:174
  23.9 5.7 %all-to-all-done.1 = bf16[16,32,128]{2,1,0:T(8,128)(2,1)S(1)} async-done(((bf16[16,32,128]{2,1,0:T(8,128)(2,1)}), bf16[16,32,128]{2,1,0:T(8,128)(2,1)S(1)}, u32[]{:S(2)}, u32[]{:S(2)}) %all-to-all-start.1) | async-done | bytes 131104 | tf_op jit(solution)/shard_map/all_to_all | solution.py:173
  29.6 0.7 %squares.1 = f32[16,1,128]{2,1,0:T(1,128)} custom-call(bf16[512,128]{1,0:T(8,128)(2,1)S(1)} %bitcast.5, f32[512,128]{1,0:T(8,128)S(1)} %gate.1.gate_ref), custom_call_target="tpu_custom_call" | custom-call | tf_op jit(solution)/shard_map/squares/pallas_call | solution.py:181
  30.3 11.5 %all-to-all-start.2 = ((f32[16,1,128]{2,1,0:T(1,128)}), f32[16,1,128]{2,1,0:T(1,128)S(1)}, u32[]{:S(2)}, u32[]{:S(2)}) async-start(f32[16,1,128]{2,1,0:T(1,128)} %squares.1), calls=%async_computation.2 | async-start | bytes 16384 | tf_op jit(solution)/shard_map/all_to_all | solution.py:188
  41.8 0.1 turn.1.x_ref
  41.9 6.8 %all-to-all-done.2.part_ref = f32[16,1,128]{2,1,0:T(1,128)S(1)} async-done(((f32[16,1,128]{2,1,0:T(1,128)}), f32[16,1,128]{2,1,0:T(1,128)S(1)}, u32[]{:S(2)}, u32[]{:S(2)}) %all-to-all-start.2) | async-done | bytes 8224 | tf_op jit(solution)/shard_map/all_to_all | solution.py:188
  48.7 1.5 %finish.1 = bf16[128,512]{1,0:T(8,128)(2,1)} custom-call(f32[128,512]{1,0:T(8,128)S(1)} %turn.1.x_ref, f32[16,1,128]{2,1,0:T(1,128)S(1)} %all-to-all-done.2.part_ref, f32[1,512]{1,0:T(1,128)} %bitcast.7), custom_call_target="tpu_custom_call" | custom-call | tf_op jit(solution)/shard_map/finish/pallas_call | solution.py:196
Async XLA Ops:
  1.9 16.1 %all-to-all-start = ((bf16[16,80,128]{2,1,0:T(8,128)(2,1)}), bf16[16,80,128]{2,1,0:T(8,128)(2,1)S(1)}, u32[]{:S(2)}, u32[]{:S(2)}) async-start(bf16[16,80,128]{2,1,0:T(8,128)(2,1)} %pack.1), calls=%async_computation | async-start | bytes 655360 | tf_op jit(solution)/shard_map/all_to_all | solution.py:157
  19.3 10.3 %all-to-all-start.1 = ((bf16[16,32,128]{2,1,0:T(8,128)(2,1)}), bf16[16,32,128]{2,1,0:T(8,128)(2,1)S(1)}, u32[]{:S(2)}, u32[]{:S(2)}) async-start(bf16[16,32,128]{2,1,0:T(8,128)(2,1)} %conv.1), calls=%async_computation.1 | async-start | bytes 262144 | tf_op jit(solution)/shard_map/all_to_all | solution.py:173
  30.3 18.4 %all-to-all-start.2 = ((f32[16,1,128]{2,1,0:T(1,128)}), f32[16,1,128]{2,1,0:T(1,128)S(1)}, u32[]{:S(2)}, u32[]{:S(2)}) async-start(f32[16,1,128]{2,1,0:T(1,128)} %squares.1), calls=%async_computation.2 | async-start | bytes 16384 | tf_op jit(solution)/shard_map/all_to_all | solution.py:188

commit v3 on v2

--- a/solution.py
+++ b/solution.py
@@ -18,18 +18,20 @@
 
 
 def pack_kernel(k_ref, v_ref, q_ref, seg_ref, out_ref):
+    index = lax.axis_index("ctx")
     for n, ref in enumerate((k_ref, v_ref)):
         value = ref[...].astype(F32).T.astype(BF16)
         out_ref[:, n * CH : (n + 1) * CH, :] = value.reshape(NB, CH, TB)
     tail = q_ref[TB - 16 :, :].astype(F32)[14:16]
-    pieces = [tail[:, n * TB : (n + 1) * TB] for n in range(4)]
-    pieces.append(jnp.broadcast_to(seg_ref[...].astype(F32), (8, TB)))
-    extra = jnp.concatenate(pieces, axis=0).astype(BF16)
-    out_ref[:, HALO:, :] = jnp.broadcast_to(extra.reshape(1, ROWS - HALO, TB), (NB, ROWS - HALO, TB))
-
-
-def band_kernel(idx_ref, fir_ref, skip_ref, taps_ref, band_ref, weight_ref, coef_ref):
-    index = idx_ref[0]
+    tail = jnp.concatenate([tail[:, n * TB : (n + 1) * TB] for n in range(4)], axis=0)
+    seg = jnp.broadcast_to(seg_ref[...].astype(F32), (8, TB))
+    for n in range(NB):
+        here = jnp.where(index == n - 1, tail, 0.0)
+        out_ref[n, HALO:, :] = jnp.concatenate([here, seg], axis=0).astype(BF16)
+
+
+def prepare_kernel(fir_ref, skip_ref, taps_ref, gain_ref, q_ref, band_ref, weight_ref, gate_ref, row_ref, coef_ref):
+    index = lax.axis_index("ctx")
     tile = pl.multiple_of((index // 4) * GW, GW)
     rows = [fir_ref[a, :, pl.ds(tile, GW)] for a in (1, 2)]
     rows.append(skip_ref[:, pl.ds(tile, GW)])
@@ -38,6 +40,8 @@
     coef = coef_ref[pl.ds(pl.multiple_of((index % 4) * CH, CH), CH), :]
     for n in range(7):
         weight_ref[n] = jnp.broadcast_to(coef[:, n : n + 1], (CH, TB))
+    row_ref[0:3] = fir_ref[0]
+    row_ref[3:4] = gain_ref[...]
 
     taps = taps_ref[...].astype(F32)
     pick = lax.broadcasted_iota(jnp.int32, taps.shape, 0) == index // 4
@@ -52,6 +56,14 @@
         rolled = pltpu.roll(piece, 0, 1, stride=1, stride_axis=0)
         band_ref[m + 1] = jnp.where(upper, rolled, before).astype(BF16)
         before = rolled
+
+    for n in range(4):
+        lanes = slice(n * TB, (n + 1) * TB)
+        here = q_ref[:, lanes].astype(F32)
+        one = jnp.where(row_at == 0, 0.0, pltpu.roll(here, 1, 0))
+        two = jnp.where(row_at <= 1, 0.0, pltpu.roll(here, 2, 0))
+        value = fir_ref[0, 0:1, lanes] * here + fir_ref[0, 1:2, lanes] * one + fir_ref[0, 2:3, lanes] * two
+        gate_ref[lanes, :] = value.T
 
 
 def conv_kernel(x_ref, band_ref, weight_ref, out_ref):
@@ -100,40 +112,31 @@
         out_ref[a] = (conv + weights[6] * product[a].astype(F32)).astype(BF16)
 
 
-def gate_kernel(idx_ref, q_ref, x_ref, fir_ref, out_ref):
-    index = idx_ref[0]
-    halo = x_ref[jnp.maximum(index - 1, 0)].astype(F32)[HALO : HALO + 8]
-    halo = jnp.where(index > 0, halo, 0.0)
+def square_kernel(u_ref, gate_ref, x_ref, row_ref, part_ref, turned_ref):
+    halo = x_ref[0, HALO:, :].astype(F32)
+    for n in range(1, NB):
+        halo = halo + x_ref[n, HALO:, :].astype(F32)
     row_at = lax.broadcasted_iota(jnp.int32, (TB, TB), 0)
+    squares = jnp.zeros((1, TB), F32)
     for n in range(4):
         lanes = slice(n * TB, (n + 1) * TB)
-        here = q_ref[:, lanes].astype(F32)
-        last, older = halo[2 * n + 1 : 2 * n + 2], halo[2 * n : 2 * n + 1]
-        one = jnp.where(row_at == 0, last, pltpu.roll(here, 1, 0))
-        two = jnp.where(row_at == 0, older, jnp.where(row_at == 1, last, pltpu.roll(here, 2, 0)))
-        value = fir_ref[0, 0:1, lanes] * here + fir_ref[0, 1:2, lanes] * one + fir_ref[0, 2:3, lanes] * two
-        out_ref[lanes, :] = value.T
-
-
-def square_kernel(u_ref, gate_ref, out_ref):
-    value = u_ref[...].astype(F32) * gate_ref[...]
-    out_ref[...] = jnp.broadcast_to(jnp.sum(value * value, axis=0, keepdims=True), (NB, 1, TB))
-
-
-def turn_kernel(u_ref, gate_ref, out_ref):
-    for n in range(4):
-        lanes = slice(n * TB, (n + 1) * TB)
-        value = u_ref[lanes, :].astype(F32) * gate_ref[lanes, :]
-        out_ref[:, lanes] = value.T
-
-
-def finish_kernel(x_ref, part_ref, gain_ref, out_ref):
+        older, last = halo[2 * n : 2 * n + 1], halo[2 * n + 1 : 2 * n + 2]
+        zero = row_ref[1:2, lanes] * last + row_ref[2:3, lanes] * older
+        one = row_ref[2:3, lanes] * last
+        extra = jnp.where(row_at == 0, zero, jnp.where(row_at == 1, one, 0.0)).T
+        gated = u_ref[lanes, :].astype(F32) * (gate_ref[lanes, :] + extra)
+        squares = squares + jnp.sum(gated * gated, axis=0, keepdims=True)
+        turned_ref[:, lanes] = gated.T * row_ref[3:4, lanes]
+    part_ref[...] = jnp.broadcast_to(squares, (NB, 1, TB))
+
+
+def finish_kernel(x_ref, part_ref, out_ref):
     squares = jnp.sum(part_ref[...], axis=0)
     scale = lax.rsqrt(squares / D + 1e-06)
     scale = jnp.broadcast_to(scale, (TB, TB)).T
     for n in range(4):
         lanes = slice(n * TB, (n + 1) * TB)
-        out_ref[:, lanes] = (x_ref[:, lanes] * scale * gain_ref[:, lanes]).astype(BF16)
+        out_ref[:, lanes] = (x_ref[:, lanes] * scale).astype(BF16)
 
 
 VM = pl.BlockSpec(memory_space=pltpu.VMEM)
@@ -146,60 +149,50 @@
 
 def on_device(q_in, k_in, v_in, fir, skip, taps, segments, gain):
     width = q_in.shape[1]
-    index = lax.axis_index("ctx").reshape(1)
     payload = pl.pallas_call(
         pack_kernel,
-        out_shape=pltpu.VMEM((NB, ROWS, TB), BF16),
-        in_specs=[VM, VM, VM, VM],
+        out_shape=jax.ShapeDtypeStruct((NB, ROWS, TB), BF16),
+        in_specs=[VM] * 4,
         out_specs=VM,
         name="pack",
     )(k_in, v_in, q_in, segments.reshape(1, TB))
     payload = lax.all_to_all(payload, "ctx", 0, 0, tiled=True)
-    band, weight = pl.pallas_call(
-        band_kernel,
-        out_shape=(pltpu.VMEM((NB + 1, TB, TB), BF16), pltpu.VMEM((7, CH, TB), F32)),
-        in_specs=[SM, VM, VM, VM],
-        out_specs=(VM, VM),
+    band, weight, gate, rows = pl.pallas_call(
+        prepare_kernel,
+        out_shape=(
+            pltpu.VMEM((NB + 1, TB, TB), BF16),
+            pltpu.VMEM((7, CH, TB), F32),
+            pltpu.VMEM((width, TB), F32),
+            pltpu.VMEM((8, width), F32),
+        ),
+        in_specs=[VM] * 5,
+        out_specs=(VM,) * 4,
         scratch_shapes=[pltpu.VMEM((GW, GW), F32)],
-        name="band",
-    )(index, fir, skip.reshape(1, width), taps)
+        name="prepare",
+    )(fir, skip.reshape(1, width), taps, gain.reshape(1, width), q_in)
     mixed = pl.pallas_call(
         conv_kernel,
         out_shape=pltpu.VMEM((NB, CH, TB), BF16),
-        in_specs=[VM, VM, VM],
+        in_specs=[VM] * 3,
         out_specs=VM,
         name="conv",
     )(keep(payload), keep(band), keep(weight))
     mixed = lax.all_to_all(mixed, "ctx", 0, 0, tiled=True).reshape(width, TB)
-    gate = pl.pallas_call(
-        gate_kernel,
-        out_shape=pltpu.VMEM((width, TB), F32),
-        in_specs=[SM, VM, VM, VM],
-        out_specs=VM,
-        name="gate",
-    )(index, q_in, keep(payload), fir)
-    part = pl.pallas_call(
+    part, turned = pl.pallas_call(
         square_kernel,
-        out_shape=pltpu.VMEM((NB, 1, TB), F32),
-        in_specs=[VM, VM],
-        out_specs=VM,
+        out_shape=(pltpu.VMEM((NB, 1, TB), F32), pltpu.VMEM((TB, width), F32)),
+        in_specs=[VM] * 4,
+        out_specs=(VM,) * 2,
         name="squares",
-    )(keep(mixed), keep(gate))
+    )(keep(mixed), keep(gate), keep(payload), keep(rows))
     part = lax.all_to_all(part, "grp", 0, 0, tiled=True)
-    turned = pl.pallas_call(
-        turn_kernel,
-        out_shape=pltpu.VMEM((TB, width), F32),
-        in_specs=[VM, VM],
-        out_specs=VM,
-        name="turn",
-    )(keep(mixed), keep(gate))
     return pl.pallas_call(
         finish_kernel,
         out_shape=jax.ShapeDtypeStruct((TB, width), BF16),
-        in_specs=[VM, VM, VM],
+        in_specs=[VM] * 2,
         out_specs=VM,
         name="finish",
-    )(keep(turned), keep(part), gain.reshape(1, width))
+    )(keep(turned), keep(part))
 
 
 def solution(mesh):

time: 50.6 us -> 47.9 us (0.947)
  blocking collectives: 0 us -> 28 us
  starting transfers between devices: 22.6 us -> 7.58 us
  waiting for transfers between devices: 19.9 us -> 7.02 us
  Pallas kernels: 7.66 us -> 4.97 us
    all_to_all x0 -> x2, blocking collectives: none -> 28 us  [the longest x1 18.5 us: on_device(): part = lax.all_to_all(part, 'grp', 0, 0, tiled=True)]
    all_to_all x2 -> x0, starting transfers between devices: 15 us -> none  [the longest x1 11.5 us: on_device(): part = lax.all_to_all(part, 'grp', 0, 0, tiled=True)]
    all_to_all x2 -> x0, waiting for transfers between devices: 12.5 us -> none  [the longest x1 6.8 us: on_device(): part = lax.all_to_all(part, 'grp', 0, 0, tiled=True)]
    pallas_call x5 -> x3, Pallas kernels: 4.9 us -> 3.56 us  [the longest x1 1.89 us: on_device(): pl.pallas_call(pack_kernel, out_shape=jax.ShapeDtypeStruct((NB, ROWS, TB)...]
    pallas_call x1, Pallas kernels: 1.47 us -> 0.78 us  [on_device(): pl.pallas_call(finish_kernel, out_shape=jax.ShapeDtypeStruct((TB, width),...]
    pallas_call x1, Pallas kernels: 1.29 us -> 0.63 us  [on_device(): pl.pallas_call(conv_kernel, out_shape=pltpu.VMEM((NB, CH, TB), BF16), in_...]
  transfers between devices with their start and end apart: 3 -> 1, of which waited for: 3 -> 1; matrix products, arithmetic and copies ran while one was open for 0% -> 0% of each run, Pallas kernels for 5% -> 3%
where the time goes in v3:
time: 47.9 us; the launch traced here: 47.6 us
  blocking collectives  28 us (58%)
  starting transfers between devices  7.58 us (16%)
  waiting for transfers between devices  7.02 us (15%)
  Pallas kernels  4.97 us (10%)
    all_to_all x1, blocking collectives, on_device(): part = lax.all_to_all(part, 'grp', 0, 0, tiled=True)  18.5 us
    all_to_all x1, blocking collectives, on_device(): mixed = lax.all_to_all(mixed, 'ctx', 0, 0, tiled=True).reshape(width, TB)  9.48 us
    all_to_all x1, starting transfers between devices, on_device(): payload = lax.all_to_all(payload, 'ctx', 0, 0, tiled=True)  7.58 us
    all_to_all x1, waiting for transfers between devices, on_device(): payload = lax.all_to_all(payload, 'ctx', 0, 0, tiled=True)  7.02 us
    pallas_call x1, Pallas kernels, on_device(): pl.pallas_call(pack_kernel, out_shape=jax.ShapeDtypeStruct((NB, ROWS, TB)...  1.89 us
    pallas_call x1, Pallas kernels, on_device(): pl.pallas_call(prepare_kernel, out_shape=(pltpu.VMEM((NB + 1, TB, TB), BF...  1.44 us
  transfers between devices with their start and end apart: 1, of which 1 were waited for; matrix products, arithmetic and copies ran while one was open for 0% of the time, Pallas kernels for 3%

profile of v3, /device:TPU:1, one launch (start us, length us, event | category | flops | bytes accessed | tf_op | source)
XLA Modules:
  0.0 47.6 jit_solution(12800467080825658650)
XLA Ops:
  0.0 1.9 %pack.1 = bf16[16,80,128]{2,1,0:T(8,128)(2,1)} custom-call(bf16[128,512]{1,0:T(8,128)(2,1)} %k_ref.1, bf16[128,512]{1,0:T(8,128)(2,1)} %v_ref.1, bf16[128,512]{1,0:T(8,128)(2,1)} %q_ref.3, s32[1,128]{1,0:T(1,128)} %bitcast.7), custom_call_target="tpu_custom_call" | custom-call | tf_op jit(solution)/shard_map/pack/pallas_call | solution.py:152
  1.9 7.6 %all-to-all-start = ((bf16[16,80,128]{2,1,0:T(8,128)(2,1)}), bf16[16,80,128]{2,1,0:T(8,128)(2,1)S(1)}, u32[]{:S(2)}, u32[]{:S(2)}) async-start(bf16[16,80,128]{2,1,0:T(8,128)(2,1)} %pack.1), calls=%async_computation | async-start | bytes 655360 | tf_op jit(solution)/shard_map/all_to_all | solution.py:159
  9.5 1.4 %prepare.1 = (bf16[17,128,128]{2,1,0:T(8,128)(2,1)S(1)}, f32[7,32,128]{2,1,0:T(8,128)S(1)}, f32[512,128]{1,0:T(8,128)S(1)}, f32[8,512]{1,0:T(8,128)S(1)}) custom-call(f32[3,3,512]{2,1,0:T(4,128)} %fir_ref.1, f32[1,512]{1,0:T(1,128)} %bitcast.5, bf16[4,2048]{1,0:T(4,128)(2,1)} %taps_ref.1, f32[1,512]{1,0:T(1,128)} %bitcast.6, bf16[128,512]{1,0:T(8,128)(2,1)} %q_ref.3), custom_call_target="tpu_custom_call" | custom-call | tf_op jit(solution)/shard_map/prepare/pallas_call | solution.py:160
  10.9 7.0 %all-to-all-done.x_ref = bf16[16,80,128]{2,1,0:T(8,128)(2,1)S(1)} async-done(((bf16[16,80,128]{2,1,0:T(8,128)(2,1)}), bf16[16,80,128]{2,1,0:T(8,128)(2,1)S(1)}, u32[]{:S(2)}, u32[]{:S(2)}) %all-to-all-start) | async-done | bytes 327712 | tf_op jit(solution)/shard_map/all_to_all | solution.py:159
  18.0 0.6 %conv.1 = bf16[16,32,128]{2,1,0:T(8,128)(2,1)S(1)} custom-call(bf16[16,80,128]{2,1,0:T(8,128)(2,1)S(1)} %all-to-all-done.x_ref, bf16[17,128,128]{2,1,0:T(8,128)(2,1)S(1)} %get-tuple-element.11.band_ref, f32[7,32,128]{2,1,0:T(8,128)S(1)} %get-tuple-element.12.weight_ref), custom_call_target="tpu_custom_call" | custom-call | tf_op jit(solution)/shard_map/conv/pallas_call | solution.py:173
  18.6 9.5 %all_to_all.15 = bf16[16,32,128]{2,1,0:T(8,128)(2,1)S(1)} all-to-all(bf16[16,32,128]{2,1,0:T(8,128)(2,1)S(1)} %conv.1), channel_id=1, replica_groups=mesh['ctx'=16,'grp'=16] {'ctx'}, dimensions={0} | all-to-all | bytes 262144 | tf_op jit(solution)/shard_map/all_to_all | solution.py:180
  28.1 0.2 squares.1
  28.3 18.5 %all_to_all.16.part_ref = f32[16,1,128]{2,1,0:T(1,128)S(1)} all-to-all(f32[16,1,128]{2,1,0:T(1,128)S(1)} %get-tuple-element.16), channel_id=1, replica_groups=mesh['ctx'=16,'grp'=16] {'grp'}, dimensions={0} | all-to-all | bytes 16384 | tf_op jit(solution)/shard_map/all_to_all | solution.py:188
  46.8 0.8 %finish.1 = bf16[128,512]{1,0:T(8,128)(2,1)} custom-call(f32[128,512]{1,0:T(8,128)S(1)} %get-tuple-element.15.x_ref, f32[16,1,128]{2,1,0:T(1,128)S(1)} %all_to_all.16.part_ref), custom_call_target="tpu_custom_call" | custom-call | tf_op jit(solution)/shard_map/finish/pallas_call | solution.py:189
Async XLA Ops:
  1.9 16.1 %all-to-all-start = ((bf16[16,80,128]{2,1,0:T(8,128)(2,1)}), bf16[16,80,128]{2,1,0:T(8,128)(2,1)S(1)}, u32[]{:S(2)}, u32[]{:S(2)}) async-start(bf16[16,80,128]{2,1,0:T(8,128)(2,1)} %pack.1), calls=%async_computation | async-start | bytes 655360 | tf_op jit(solution)/shard_map/all_to_all | solution.py:159

commit v4 on v3

--- a/solution.py
+++ b/solution.py
@@ -17,7 +17,10 @@
 BF16 = jnp.bfloat16
 
 
-def pack_kernel(k_ref, v_ref, q_ref, seg_ref, out_ref):
+def prepare_kernel(
+    k_ref, v_ref, q_ref, seg_ref, fir_ref, skip_ref, taps_ref, gain_ref,
+    out_ref, band_ref, weight_ref, gate_ref, row_ref, coef_ref,
+):
     index = lax.axis_index("ctx")
     for n, ref in enumerate((k_ref, v_ref)):
         value = ref[...].astype(F32).T.astype(BF16)
@@ -29,9 +32,6 @@
         here = jnp.where(index == n - 1, tail, 0.0)
         out_ref[n, HALO:, :] = jnp.concatenate([here, seg], axis=0).astype(BF16)
 
-
-def prepare_kernel(fir_ref, skip_ref, taps_ref, gain_ref, q_ref, band_ref, weight_ref, gate_ref, row_ref, coef_ref):
-    index = lax.axis_index("ctx")
     tile = pl.multiple_of((index // 4) * GW, GW)
     rows = [fir_ref[a, :, pl.ds(tile, GW)] for a in (1, 2)]
     rows.append(skip_ref[:, pl.ds(tile, GW)])
@@ -149,27 +149,24 @@
 
 def on_device(q_in, k_in, v_in, fir, skip, taps, segments, gain):
     width = q_in.shape[1]
-    payload = pl.pallas_call(
-        pack_kernel,
-        out_shape=jax.ShapeDtypeStruct((NB, ROWS, TB), BF16),
-        in_specs=[VM] * 4,
-        out_specs=VM,
-        name="pack",
-    )(k_in, v_in, q_in, segments.reshape(1, TB))
-    payload = lax.all_to_all(payload, "ctx", 0, 0, tiled=True)
-    band, weight, gate, rows = pl.pallas_call(
+    payload, band, weight, gate, rows = pl.pallas_call(
         prepare_kernel,
         out_shape=(
+            pltpu.VMEM((NB, ROWS, TB), BF16),
             pltpu.VMEM((NB + 1, TB, TB), BF16),
             pltpu.VMEM((7, CH, TB), F32),
             pltpu.VMEM((width, TB), F32),
             pltpu.VMEM((8, width), F32),
         ),
-        in_specs=[VM] * 5,
-        out_specs=(VM,) * 4,
+        in_specs=[VM] * 8,
+        out_specs=(VM,) * 5,
         scratch_shapes=[pltpu.VMEM((GW, GW), F32)],
         name="prepare",
-    )(fir, skip.reshape(1, width), taps, gain.reshape(1, width), q_in)
+    )(
+        k_in, v_in, q_in, segments.reshape(1, TB),
+        fir, skip.reshape(1, width), taps, gain.reshape(1, width),
+    )
+    payload = lax.all_to_all(payload, "ctx", 0, 0, tiled=True)
     mixed = pl.pallas_call(
         conv_kernel,
         out_shape=pltpu.VMEM((NB, CH, TB), BF16),

time: 47.9 us -> 47.4 us (0.990)
  blocking collectives: 28 us -> 43.9 us
  starting transfers between devices: 7.58 us -> 0 us
  waiting for transfers between devices: 7.02 us -> 0 us
  Pallas kernels: 4.97 us -> 3.33 us
    all_to_all x0 -> x1, blocking collectives: none -> 15.9 us  [on_device(): payload = lax.all_to_all(payload, 'ctx', 0, 0, tiled=True)]
    all_to_all x1 -> x0, starting transfers between devices: 7.58 us -> none  [on_device(): payload = lax.all_to_all(payload, 'ctx', 0, 0, tiled=True)]
    all_to_all x1 -> x0, waiting for transfers between devices: 7.02 us -> none  [on_device(): payload = lax.all_to_all(payload, 'ctx', 0, 0, tiled=True)]
    pallas_call x2 -> x1, Pallas kernels: 3.33 us -> 1.7 us  [on_device(): pl.pallas_call(prepare_kernel, out_shape=(pltpu.VMEM((NB, ROWS, TB), BF16...]
  transfers between devices with their start and end apart: 1 -> 0, of which waited for: 1 -> 0; matrix products, arithmetic and copies ran while one was open for 0% -> 0% of each run, Pallas kernels for 3% -> 0%
where the time goes in v4:
time: 47.4 us; the launch traced here: 47.2 us
  blocking collectives  43.9 us (93%)
  Pallas kernels  3.33 us (7%)
    all_to_all x1, blocking collectives, on_device(): part = lax.all_to_all(part, 'grp', 0, 0, tiled=True)  18.5 us
    all_to_all x1, blocking collectives, on_device(): payload = lax.all_to_all(payload, 'ctx', 0, 0, tiled=True)  15.9 us
    all_to_all x1, blocking collectives, on_device(): mixed = lax.all_to_all(mixed, 'ctx', 0, 0, tiled=True).reshape(width, TB)  9.48 us
    pallas_call x1, Pallas kernels, on_device(): pl.pallas_call(prepare_kernel, out_shape=(pltpu.VMEM((NB, ROWS, TB), BF16...  1.7 us

profile of v4, /device:TPU:1, one launch (start us, length us, event | category | flops | bytes accessed | tf_op | source)
XLA Modules:
  0.0 47.2 jit_solution(934871101125778183)
XLA Ops:
  0.0 1.7 %prepare.1 = (bf16[16,80,128]{2,1,0:T(8,128)(2,1)S(1)}, bf16[17,128,128]{2,1,0:T(8,128)(2,1)S(1)}, f32[7,32,128]{2,1,0:T(8,128)S(1)}, f32[512,128]{1,0:T(8,128)S(1)}, f32[8,512]{1,0:T(8,128)S(1)}) custom-call(bf16[128,512]{1,0:T(8,128)(2,1)} %k_ref.1, bf16[128,512]{1,0:T(8,128)(2,1)} %v_ref.1, bf16[128,512]{1,0:T(8,128)(2,1)} %q_ref.1, s32[1,128]{1,0:T(1,128)} %bitcast.7, ...), custom_call_target="tpu_custom_call" | custom-call | tf_op jit(solution)/shard_map/prepare/pallas_call | solution.py:152
  1.7 15.9 %all_to_all.15.x_ref = bf16[16,80,128]{2,1,0:T(8,128)(2,1)S(1)} all-to-all(bf16[16,80,128]{2,1,0:T(8,128)(2,1)S(1)} %get-tuple-element.12), channel_id=1, replica_groups=mesh['ctx'=16,'grp'=16] {'ctx'}, dimensions={0} | all-to-all | bytes 655360 | tf_op jit(solution)/shard_map/all_to_all | solution.py:169
  17.6 0.6 %conv.1 = bf16[16,32,128]{2,1,0:T(8,128)(2,1)S(1)} custom-call(bf16[16,80,128]{2,1,0:T(8,128)(2,1)S(1)} %all_to_all.15.x_ref, bf16[17,128,128]{2,1,0:T(8,128)(2,1)S(1)} %get-tuple-element.13.band_ref, f32[7,32,128]{2,1,0:T(8,128)S(1)} %get-tuple-element.14.weight_ref), custom_call_target="tpu_custom_call" | custom-call | tf_op jit(solution)/shard_map/conv/pallas_call | solution.py:170
  18.2 9.5 %all_to_all.16 = bf16[16,32,128]{2,1,0:T(8,128)(2,1)S(1)} all-to-all(bf16[16,32,128]{2,1,0:T(8,128)(2,1)S(1)} %conv.1), channel_id=1, replica_groups=mesh['ctx'=16,'grp'=16] {'ctx'}, dimensions={0} | all-to-all | bytes 262144 | tf_op jit(solution)/shard_map/all_to_all | solution.py:177
  27.7 0.2 squares.1
  27.9 18.5 %all_to_all.17.part_ref = f32[16,1,128]{2,1,0:T(1,128)S(1)} all-to-all(f32[16,1,128]{2,1,0:T(1,128)S(1)} %get-tuple-element.18), channel_id=1, replica_groups=mesh['ctx'=16,'grp'=16] {'grp'}, dimensions={0} | all-to-all | bytes 16384 | tf_op jit(solution)/shard_map/all_to_all | solution.py:185
  46.4 0.8 %finish.1 = bf16[128,512]{1,0:T(8,128)(2,1)} custom-call(f32[128,512]{1,0:T(8,128)S(1)} %get-tuple-element.17.x_ref, f32[16,1,128]{2,1,0:T(1,128)S(1)} %all_to_all.17.part_ref), custom_call_target="tpu_custom_call" | custom-call | tf_op jit(solution)/shard_map/finish/pallas_call | solution.py:186

commit v5 on v4

--- a/solution.py
+++ b/solution.py
@@ -10,11 +10,24 @@
 NB = 16
 TB = 128
 CH = 32
-HALO = 2 * CH
-SEG = HALO + 8
+HALO = CH
+EDGE = HALO + 8
 ROWS = HALO + 16
 F32 = jnp.float32
 BF16 = jnp.bfloat16
+
+
+def one_hot(rows, by):
+    row_at = lax.broadcasted_iota(jnp.int32, (rows, TB), 0)
+    col_at = lax.broadcasted_iota(jnp.int32, (rows, TB), 1)
+    return jnp.where(row_at == col_at + by, 1.0, 0.0).astype(BF16)
+
+
+def fir_filter(ref, fir_ref, which, lanes, shifts):
+    value = ref[:, lanes]
+    moved = [jnp.dot(shift, value, preferred_element_type=F32) for shift in shifts]
+    taps = [fir_ref[which, n : n + 1, lanes] for n in range(3)]
+    return taps[0] * value.astype(F32) + taps[1] * moved[0] + taps[2] * moved[1]
 
 
 def prepare_kernel(
@@ -22,15 +35,28 @@
     out_ref, band_ref, weight_ref, gate_ref, row_ref, coef_ref,
 ):
     index = lax.axis_index("ctx")
-    for n, ref in enumerate((k_ref, v_ref)):
-        value = ref[...].astype(F32).T.astype(BF16)
-        out_ref[:, n * CH : (n + 1) * CH, :] = value.reshape(NB, CH, TB)
+    row_at = lax.broadcasted_iota(jnp.int32, (TB, TB), 0)
+    col_at = lax.broadcasted_iota(jnp.int32, (TB, TB), 1)
+    same, shifts = one_hot(TB, 0), (one_hot(TB, 1), one_hot(TB, 2))
+    first = jnp.sum(jnp.where(seg_ref[...] == 0, 1.0, 0.0), axis=1, keepdims=True)
     tail = q_ref[TB - 16 :, :].astype(F32)[14:16]
     tail = jnp.concatenate([tail[:, n * TB : (n + 1) * TB] for n in range(4)], axis=0)
-    seg = jnp.broadcast_to(seg_ref[...].astype(F32), (8, TB))
-    for n in range(NB):
-        here = jnp.where(index == n - 1, tail, 0.0)
-        out_ref[n, HALO:, :] = jnp.concatenate([here, seg], axis=0).astype(BF16)
+    heads = [ref[0:16, :].astype(F32)[0:2] for ref in (k_ref, v_ref)]
+    tails = [ref[TB - 16 :, :].astype(F32)[14:16] for ref in (k_ref, v_ref)]
+    edges = jnp.concatenate([heads[0], tails[0], heads[1], tails[1]], axis=0)
+    for n in range(4):
+        lanes = slice(n * TB, (n + 1) * TB)
+        value = fir_filter(k_ref, fir_ref, 1, lanes, shifts) * fir_filter(v_ref, fir_ref, 2, lanes, shifts)
+        value = lax.dot_general(
+            same, value.astype(BF16), (((1,), (1,)), ((), ())), preferred_element_type=F32
+        )
+        value = jnp.where(col_at == 0, first, value)
+        out_ref[4 * n : 4 * n + 4, 0:CH, :] = value.astype(BF16).reshape(4, CH, TB)
+        gate_ref[lanes, :] = fir_filter(q_ref, fir_ref, 0, lanes, shifts).T
+        for m in range(4):
+            here = jnp.where(index == 4 * n + m - 1, tail, 0.0)
+            edge = pltpu.roll(edges[:, lanes], (TB - m * CH) % TB, 1) if m else edges[:, lanes]
+            out_ref[4 * n + m, HALO:, :] = jnp.concatenate([here, edge], axis=0).astype(BF16)
 
     tile = pl.multiple_of((index // 4) * GW, GW)
     rows = [fir_ref[a, :, pl.ds(tile, GW)] for a in (1, 2)]
@@ -46,8 +72,6 @@
     taps = taps_ref[...].astype(F32)
     pick = lax.broadcasted_iota(jnp.int32, taps.shape, 0) == index // 4
     row = jnp.sum(jnp.where(pick, taps, 0.0), axis=0, keepdims=True)
-    row_at = lax.broadcasted_iota(jnp.int32, (TB, TB), 0)
-    col_at = lax.broadcasted_iota(jnp.int32, (TB, TB), 1)
     upper = col_at >= row_at
     before = jnp.zeros((TB, TB), F32)
     band_ref[0] = before.astype(BF16)
@@ -57,38 +81,39 @@
         band_ref[m + 1] = jnp.where(upper, rolled, before).astype(BF16)
         before = rolled
 
-    for n in range(4):
-        lanes = slice(n * TB, (n + 1) * TB)
-        here = q_ref[:, lanes].astype(F32)
-        one = jnp.where(row_at == 0, 0.0, pltpu.roll(here, 1, 0))
-        two = jnp.where(row_at <= 1, 0.0, pltpu.roll(here, 2, 0))
-        value = fir_ref[0, 0:1, lanes] * here + fir_ref[0, 1:2, lanes] * one + fir_ref[0, 2:3, lanes] * two
-        gate_ref[lanes, :] = value.T
-
 
 def conv_kernel(x_ref, band_ref, weight_ref, out_ref):
     lane = lax.broadcasted_iota(jnp.int32, (CH, TB), 1)
-    weights = [weight_ref[n] for n in range(7)]
-
-    def filtered(a, which):
-        lo = which * CH
-        here = x_ref[a, lo : lo + CH, :].astype(F32)
-        past = x_ref[a - 1, lo : lo + CH, :].astype(F32) if a else jnp.zeros_like(here)
-        one = jnp.where(lane >= 1, pltpu.roll(here, 1, 1), pltpu.roll(past, 1, 1))
-        two = jnp.where(lane >= 2, pltpu.roll(here, 2, 1), pltpu.roll(past, 2, 1))
-        return weights[3 * which] * here + weights[3 * which + 1] * one + weights[3 * which + 2] * two
-
-    product, second = [], []
+    edges = jnp.concatenate([x_ref[a, HALO:, :].astype(F32)[8:16] for a in range(NB)], axis=0).T[0:CH]
+
+    def ahead(by):
+        return pltpu.roll(edges, TB - by, 1) if by else edges
+
+    def behind(by):
+        return jnp.where(lane < 8, 0.0, pltpu.roll(edges, by, 1))
+
+    def pair(at, which):
+        w = [weight_ref[3 * which + n] for n in range(3)]
+        zero, one, older, last = ahead(at), ahead(at + 1), behind(6 - at), behind(5 - at)
+        return w[0] * zero + w[1] * last + w[2] * older, w[0] * one + w[1] * zero + w[2] * last
+
+    k_zero, k_one = pair(0, 0)
+    v_zero, v_one = pair(4, 1)
+    fixed = jnp.where(lane % 8 == 0, k_zero * v_zero, pltpu.roll(k_one * v_one, 1, 1))
+
+    product, second, masks = [], [], []
     for a in range(NB):
-        value = (filtered(a, 0) * filtered(a, 1)).astype(BF16)
-        product.append(value)
-        mask = x_ref[a, SEG : SEG + 1, :]
-        second.append(value * mask)
+        value = x_ref[a, 0:CH, :].astype(F32)
+        mask = lane.astype(F32) >= jnp.broadcast_to(value[:, 0:1], (CH, TB))
+        value = jnp.where(lane < 2, pltpu.roll(fixed, (TB - 8 * a) % TB, 1) if a else fixed, value)
+        product.append(value.astype(BF16))
+        second.append(jnp.where(mask, value, 0.0).astype(BF16))
+        masks.append(mask)
     pairs = NB // 2
     lhs = []
     for source in (product, second):
-        for pair in range(pairs):
-            lhs.append(jnp.concatenate([source[2 * pair], source[2 * pair + 1]], axis=1))
+        for at in range(pairs):
+            lhs.append(jnp.concatenate([source[2 * at], source[2 * at + 1]], axis=1))
     total = [None] * (2 * pairs)
     for d in range(pairs):
         matrix = jnp.concatenate(
@@ -107,9 +132,8 @@
                 total[at] = piece if total[at] is None else total[at] + piece
     for a in range(NB):
         side = slice((a % 2) * TB, (a % 2 + 1) * TB)
-        mask = x_ref[a, SEG : SEG + 1, :].astype(F32)
-        conv = jnp.where(mask > 0.5, total[pairs + a // 2][:, side], total[a // 2][:, side])
-        out_ref[a] = (conv + weights[6] * product[a].astype(F32)).astype(BF16)
+        conv = jnp.where(masks[a], total[pairs + a // 2][:, side], total[a // 2][:, side])
+        out_ref[a] = (conv + weight_ref[6] * product[a].astype(F32)).astype(BF16)
 
 
 def square_kernel(u_ref, gate_ref, x_ref, row_ref, part_ref, turned_ref):

time: 47.4 us -> 46.9 us (0.989)
  blocking collectives: 43.9 us -> 42.9 us
    all_to_all x1, blocking collectives: 15.9 us -> 14.6 us  [on_device(): payload = lax.all_to_all(payload, 'ctx', 0, 0, tiled=True)]
where the time goes in v5:
time: 46.9 us; the launch traced here: 46.7 us
  blocking collectives  42.9 us (91%)
  Pallas kernels  3.75 us (8%)
    all_to_all x1, blocking collectives, on_device(): part = lax.all_to_all(part, 'grp', 0, 0, tiled=True)  18.5 us
    all_to_all x1, blocking collectives, on_device(): payload = lax.all_to_all(payload, 'ctx', 0, 0, tiled=True)  14.6 us
    all_to_all x1, blocking collectives, on_device(): mixed = lax.all_to_all(mixed, 'ctx', 0, 0, tiled=True).reshape(width, TB)  9.84 us
    pallas_call x1, Pallas kernels, on_device(): pl.pallas_call(prepare_kernel, out_shape=(pltpu.VMEM((NB, ROWS, TB), BF16...  2.01 us

profile of v5, /device:TPU:1, one launch (start us, length us, event | category | flops | bytes accessed | tf_op | source)
XLA Modules:
  0.0 46.7 jit_solution(5442118630673303951)
XLA Ops:
  0.0 2.0 %prepare.1 = (bf16[16,48,128]{2,1,0:T(8,128)(2,1)S(1)}, bf16[17,128,128]{2,1,0:T(8,128)(2,1)S(1)}, f32[7,32,128]{2,1,0:T(8,128)S(1)}, f32[512,128]{1,0:T(8,128)S(1)}, f32[8,512]{1,0:T(8,128)S(1)}) custom-call(bf16[128,512]{1,0:T(8,128)(2,1)} %k_ref.1, bf16[128,512]{1,0:T(8,128)(2,1)} %v_ref.1, bf16[128,512]{1,0:T(8,128)(2,1)} %q_ref.1, s32[1,128]{1,0:T(1,128)} %bitcast.7, ...), custom_call_target="tpu_custom_call" | custom-call | tf_op jit(solution)/shard_map/prepare/pallas_call | solution.py:176
  2.0 14.6 %all_to_all.15.x_ref = bf16[16,48,128]{2,1,0:T(8,128)(2,1)S(1)} all-to-all(bf16[16,48,128]{2,1,0:T(8,128)(2,1)S(1)} %get-tuple-element.12), channel_id=1, replica_groups=mesh['ctx'=16,'grp'=16] {'ctx'}, dimensions={0} | all-to-all | bytes 393216 | tf_op jit(solution)/shard_map/all_to_all | solution.py:193
  16.6 0.7 %conv.1 = bf16[16,32,128]{2,1,0:T(8,128)(2,1)S(1)} custom-call(bf16[16,48,128]{2,1,0:T(8,128)(2,1)S(1)} %all_to_all.15.x_ref, bf16[17,128,128]{2,1,0:T(8,128)(2,1)S(1)} %get-tuple-element.13.band_ref, f32[7,32,128]{2,1,0:T(8,128)S(1)} %get-tuple-element.14.weight_ref), custom_call_target="tpu_custom_call" | custom-call | tf_op jit(solution)/shard_map/conv/pallas_call | solution.py:194
  17.3 9.8 %all_to_all.16 = bf16[16,32,128]{2,1,0:T(8,128)(2,1)S(1)} all-to-all(bf16[16,32,128]{2,1,0:T(8,128)(2,1)S(1)} %conv.1), channel_id=1, replica_groups=mesh['ctx'=16,'grp'=16] {'ctx'}, dimensions={0} | all-to-all | bytes 262144 | tf_op jit(solution)/shard_map/all_to_all | solution.py:201
  27.2 0.2 squares.1
  27.4 18.5 %all_to_all.17.part_ref = f32[16,1,128]{2,1,0:T(1,128)S(1)} all-to-all(f32[16,1,128]{2,1,0:T(1,128)S(1)} %get-tuple-element.18), channel_id=1, replica_groups=mesh['ctx'=16,'grp'=16] {'grp'}, dimensions={0} | all-to-all | bytes 16384 | tf_op jit(solution)/shard_map/all_to_all | solution.py:209
  45.9 0.8 %finish.1 = bf16[128,512]{1,0:T(8,128)(2,1)} custom-call(f32[128,512]{1,0:T(8,128)S(1)} %get-tuple-element.17.x_ref, f32[16,1,128]{2,1,0:T(1,128)S(1)} %all_to_all.17.part_ref), custom_call_target="tpu_custom_call" | custom-call | tf_op jit(solution)/shard_map/finish/pallas_call | solution.py:210

commit v6 on v5

--- a/solution.py
+++ b/solution.py
@@ -17,17 +17,13 @@
 BF16 = jnp.bfloat16
 
 
-def one_hot(rows, by):
-    row_at = lax.broadcasted_iota(jnp.int32, (rows, TB), 0)
-    col_at = lax.broadcasted_iota(jnp.int32, (rows, TB), 1)
-    return jnp.where(row_at == col_at + by, 1.0, 0.0).astype(BF16)
-
-
-def fir_filter(ref, fir_ref, which, lanes, shifts):
-    value = ref[:, lanes]
-    moved = [jnp.dot(shift, value, preferred_element_type=F32) for shift in shifts]
+def fir_filter(ref, fir_ref, which, lanes, row_at=None):
+    value = ref[:, lanes].astype(F32)
+    one, two = pltpu.roll(value, 1, 0), pltpu.roll(value, 2, 0)
+    if row_at is not None:
+        one, two = jnp.where(row_at == 0, 0.0, one), jnp.where(row_at <= 1, 0.0, two)
     taps = [fir_ref[which, n : n + 1, lanes] for n in range(3)]
-    return taps[0] * value.astype(F32) + taps[1] * moved[0] + taps[2] * moved[1]
+    return taps[0] * value + taps[1] * one + taps[2] * two
 
 
 def prepare_kernel(
@@ -37,7 +33,7 @@
     index = lax.axis_index("ctx")
     row_at = lax.broadcasted_iota(jnp.int32, (TB, TB), 0)
     col_at = lax.broadcasted_iota(jnp.int32, (TB, TB), 1)
-    same, shifts = one_hot(TB, 0), (one_hot(TB, 1), one_hot(TB, 2))
+    same = jnp.where(row_at == col_at, 1.0, 0.0).astype(BF16)
     first = jnp.sum(jnp.where(seg_ref[...] == 0, 1.0, 0.0), axis=1, keepdims=True)
     tail = q_ref[TB - 16 :, :].astype(F32)[14:16]
     tail = jnp.concatenate([tail[:, n * TB : (n + 1) * TB] for n in range(4)], axis=0)
@@ -46,13 +42,13 @@
     edges = jnp.concatenate([heads[0], tails[0], heads[1], tails[1]], axis=0)
     for n in range(4):
         lanes = slice(n * TB, (n + 1) * TB)
-        value = fir_filter(k_ref, fir_ref, 1, lanes, shifts) * fir_filter(v_ref, fir_ref, 2, lanes, shifts)
+        value = fir_filter(k_ref, fir_ref, 1, lanes) * fir_filter(v_ref, fir_ref, 2, lanes)
         value = lax.dot_general(
             same, value.astype(BF16), (((1,), (1,)), ((), ())), preferred_element_type=F32
         )
         value = jnp.where(col_at == 0, first, value)
         out_ref[4 * n : 4 * n + 4, 0:CH, :] = value.astype(BF16).reshape(4, CH, TB)
-        gate_ref[lanes, :] = fir_filter(q_ref, fir_ref, 0, lanes, shifts).T
+        gate_ref[lanes, :] = fir_filter(q_ref, fir_ref, 0, lanes, row_at).T
         for m in range(4):
             here = jnp.where(index == 4 * n + m - 1, tail, 0.0)
             edge = pltpu.roll(edges[:, lanes], (TB - m * CH) % TB, 1) if m else edges[:, lanes]
@@ -101,20 +97,21 @@
     v_zero, v_one = pair(4, 1)
     fixed = jnp.where(lane % 8 == 0, k_zero * v_zero, pltpu.roll(k_one * v_one, 1, 1))
 
-    product, second, masks = [], [], []
+    product, second, masks, after = [], [], [], []
     for a in range(NB):
         value = x_ref[a, 0:CH, :].astype(F32)
-        mask = lane.astype(F32) >= jnp.broadcast_to(value[:, 0:1], (CH, TB))
+        first = jnp.broadcast_to(value[:, 0:1], (CH, TB))
+        mask = lane.astype(F32) >= first
+        if a % 2 == 0:
+            after.append(jnp.concatenate([first, first], axis=1) == 0.0)
         value = jnp.where(lane < 2, pltpu.roll(fixed, (TB - 8 * a) % TB, 1) if a else fixed, value)
         product.append(value.astype(BF16))
         second.append(jnp.where(mask, value, 0.0).astype(BF16))
         masks.append(mask)
     pairs = NB // 2
-    lhs = []
-    for source in (product, second):
-        for at in range(pairs):
-            lhs.append(jnp.concatenate([source[2 * at], source[2 * at + 1]], axis=1))
-    total = [None] * (2 * pairs)
+    full = [jnp.concatenate(product[2 * at : 2 * at + 2], axis=1) for at in range(pairs)]
+    late = [jnp.concatenate(second[2 * at : 2 * at + 2], axis=1) for at in range(pairs)]
+    total = [None] * pairs
     for d in range(pairs):
         matrix = jnp.concatenate(
             [
@@ -123,16 +120,21 @@
             ],
             axis=0,
         )
-        used = lhs[: pairs - d] + lhs[pairs : 2 * pairs - d]
+        if d:
+            used = [jnp.where(after[n + d], late[n], full[n]) for n in range(pairs - d)]
+        else:
+            used = full + late
         result = jnp.dot(jnp.concatenate(used, axis=0), matrix, preferred_element_type=F32)
-        for n in range(pairs - d):
-            for half in range(2):
-                piece = result[(half * (pairs - d) + n) * CH :][:CH]
-                at = half * pairs + n + d
-                total[at] = piece if total[at] is None else total[at] + piece
+        pieces = [result[n * CH : (n + 1) * CH] for n in range(len(used))]
+        if d:
+            for n in range(pairs - d):
+                total[n + d] = total[n + d] + pieces[n]
+        else:
+            total, alone = pieces[:pairs], pieces[pairs:]
     for a in range(NB):
         side = slice((a % 2) * TB, (a % 2 + 1) * TB)
-        conv = jnp.where(masks[a], total[pairs + a // 2][:, side], total[a // 2][:, side])
+        inner = masks[a] & ~after[a // 2][:, side]
+        conv = jnp.where(inner, alone[a // 2][:, side], total[a // 2][:, side])
         out_ref[a] = (conv + weight_ref[6] * product[a].astype(F32)).astype(BF16)
 
 

time: 46.9 us -> 46.5 us (level)
  no operation moved by 1% of the time
where the time goes in v6:
time: 46.5 us; the launch traced here: 46.3 us
  blocking collectives  42.9 us (92%)
  Pallas kernels  3.31 us (7%)
    all_to_all x1, blocking collectives, on_device(): part = lax.all_to_all(part, 'grp', 0, 0, tiled=True)  18.5 us
    all_to_all x1, blocking collectives, on_device(): payload = lax.all_to_all(payload, 'ctx', 0, 0, tiled=True)  14.6 us
    all_to_all x1, blocking collectives, on_device(): mixed = lax.all_to_all(mixed, 'ctx', 0, 0, tiled=True).reshape(width, TB)  9.84 us
    pallas_call x1, Pallas kernels, on_device(): pl.pallas_call(prepare_kernel, out_shape=(pltpu.VMEM((NB, ROWS, TB), BF16...  1.65 us

profile of v6, /device:TPU:1, one launch (start us, length us, event | category | flops | bytes accessed | tf_op | source)
XLA Modules:
  0.0 46.3 jit_solution(1157676412578322885)
XLA Ops:
  0.0 1.6 %prepare.1 = (bf16[16,48,128]{2,1,0:T(8,128)(2,1)S(1)}, bf16[17,128,128]{2,1,0:T(8,128)(2,1)S(1)}, f32[7,32,128]{2,1,0:T(8,128)S(1)}, f32[512,128]{1,0:T(8,128)S(1)}, f32[8,512]{1,0:T(8,128)S(1)}) custom-call(bf16[128,512]{1,0:T(8,128)(2,1)} %k_ref.1, bf16[128,512]{1,0:T(8,128)(2,1)} %v_ref.1, bf16[128,512]{1,0:T(8,128)(2,1)} %q_ref.1, s32[1,128]{1,0:T(1,128)} %bitcast.7, ...), custom_call_target="tpu_custom_call" | custom-call | tf_op jit(solution)/shard_map/prepare/pallas_call | solution.py:178
  1.7 14.6 %all_to_all.15.x_ref = bf16[16,48,128]{2,1,0:T(8,128)(2,1)S(1)} all-to-all(bf16[16,48,128]{2,1,0:T(8,128)(2,1)S(1)} %get-tuple-element.12), channel_id=1, replica_groups=mesh['ctx'=16,'grp'=16] {'ctx'}, dimensions={0} | all-to-all | bytes 393216 | tf_op jit(solution)/shard_map/all_to_all | solution.py:195
  16.2 0.7 %conv.1 = bf16[16,32,128]{2,1,0:T(8,128)(2,1)S(1)} custom-call(bf16[16,48,128]{2,1,0:T(8,128)(2,1)S(1)} %all_to_all.15.x_ref, bf16[17,128,128]{2,1,0:T(8,128)(2,1)S(1)} %get-tuple-element.13.band_ref, f32[7,32,128]{2,1,0:T(8,128)S(1)} %get-tuple-element.14.weight_ref), custom_call_target="tpu_custom_call" | custom-call | tf_op jit(solution)/shard_map/conv/pallas_call | solution.py:196
  16.9 9.8 %all_to_all.16 = bf16[16,32,128]{2,1,0:T(8,128)(2,1)S(1)} all-to-all(bf16[16,32,128]{2,1,0:T(8,128)(2,1)S(1)} %conv.1), channel_id=1, replica_groups=mesh['ctx'=16,'grp'=16] {'ctx'}, dimensions={0} | all-to-all | bytes 262144 | tf_op jit(solution)/shard_map/all_to_all | solution.py:203
  26.7 0.2 squares.1
  27.0 18.5 %all_to_all.17.part_ref = f32[16,1,128]{2,1,0:T(1,128)S(1)} all-to-all(f32[16,1,128]{2,1,0:T(1,128)S(1)} %get-tuple-element.18), channel_id=1, replica_groups=mesh['ctx'=16,'grp'=16] {'grp'}, dimensions={0} | all-to-all | bytes 16384 | tf_op jit(solution)/shard_map/all_to_all | solution.py:211
  45.5 0.8 %finish.1 = bf16[128,512]{1,0:T(8,128)(2,1)} custom-call(f32[128,512]{1,0:T(8,128)S(1)} %get-tuple-element.17.x_ref, f32[16,1,128]{2,1,0:T(1,128)S(1)} %all_to_all.17.part_ref), custom_call_target="tpu_custom_call" | custom-call | tf_op jit(solution)/shard_map/finish/pallas_call | solution.py:212

commit v7 on v6

--- a/solution.py
+++ b/solution.py
@@ -13,6 +13,9 @@
 HALO = CH
 EDGE = HALO + 8
 ROWS = HALO + 16
+CTX_ORDER = [(10 + n) % NB for n in range(NB)]
+GRP_ORDER = [(9 + n) % NB for n in range(NB)]
+PLACE = [CTX_ORDER.index(a) for a in range(NB)]
 F32 = jnp.float32
 BF16 = jnp.bfloat16
 
@@ -46,13 +49,14 @@
         value = lax.dot_general(
             same, value.astype(BF16), (((1,), (1,)), ((), ())), preferred_element_type=F32
         )
-        value = jnp.where(col_at == 0, first, value)
-        out_ref[4 * n : 4 * n + 4, 0:CH, :] = value.astype(BF16).reshape(4, CH, TB)
+        value = jnp.where(col_at == 0, first, value).astype(BF16)
         gate_ref[lanes, :] = fir_filter(q_ref, fir_ref, 0, lanes, row_at).T
         for m in range(4):
             here = jnp.where(index == 4 * n + m - 1, tail, 0.0)
             edge = pltpu.roll(edges[:, lanes], (TB - m * CH) % TB, 1) if m else edges[:, lanes]
-            out_ref[4 * n + m, HALO:, :] = jnp.concatenate([here, edge], axis=0).astype(BF16)
+            at = PLACE[4 * n + m]
+            out_ref[at, 0:CH, :] = value[m * CH : (m + 1) * CH]
+            out_ref[at, HALO:, :] = jnp.concatenate([here, edge], axis=0).astype(BF16)
 
     tile = pl.multiple_of((index // 4) * GW, GW)
     rows = [fir_ref[a, :, pl.ds(tile, GW)] for a in (1, 2)]
@@ -80,7 +84,7 @@
 
 def conv_kernel(x_ref, band_ref, weight_ref, out_ref):
     lane = lax.broadcasted_iota(jnp.int32, (CH, TB), 1)
-    edges = jnp.concatenate([x_ref[a, HALO:, :].astype(F32)[8:16] for a in range(NB)], axis=0).T[0:CH]
+    edges = jnp.concatenate([x_ref[PLACE[a], HALO:, :].astype(F32)[8:16] for a in range(NB)], axis=0).T[0:CH]
 
     def ahead(by):
         return pltpu.roll(edges, TB - by, 1) if by else edges
@@ -99,7 +103,7 @@
 
     product, second, masks, after = [], [], [], []
     for a in range(NB):
-        value = x_ref[a, 0:CH, :].astype(F32)
+        value = x_ref[PLACE[a], 0:CH, :].astype(F32)
         first = jnp.broadcast_to(value[:, 0:1], (CH, TB))
         mask = lane.astype(F32) >= first
         if a % 2 == 0:
@@ -135,7 +139,7 @@
         side = slice((a % 2) * TB, (a % 2 + 1) * TB)
         inner = masks[a] & ~after[a // 2][:, side]
         conv = jnp.where(inner, alone[a // 2][:, side], total[a // 2][:, side])
-        out_ref[a] = (conv + weight_ref[6] * product[a].astype(F32)).astype(BF16)
+        out_ref[PLACE[a]] = (conv + weight_ref[6] * product[a].astype(F32)).astype(BF16)
 
 
 def square_kernel(u_ref, gate_ref, x_ref, row_ref, part_ref, turned_ref):
@@ -150,7 +154,8 @@
         zero = row_ref[1:2, lanes] * last + row_ref[2:3, lanes] * older
         one = row_ref[2:3, lanes] * last
         extra = jnp.where(row_at == 0, zero, jnp.where(row_at == 1, one, 0.0)).T
-        gated = u_ref[lanes, :].astype(F32) * (gate_ref[lanes, :] + extra)
+        mixed = jnp.concatenate([u_ref[PLACE[4 * n + m]] for m in range(4)], axis=0)
+        gated = mixed.astype(F32) * (gate_ref[lanes, :] + extra)
         squares = squares + jnp.sum(gated * gated, axis=0, keepdims=True)
         turned_ref[:, lanes] = gated.T * row_ref[3:4, lanes]
     part_ref[...] = jnp.broadcast_to(squares, (NB, 1, TB))
@@ -171,6 +176,10 @@
 
 def keep(value):
     return pltpu.with_memory_space_constraint(value, pltpu.VMEM)
+
+
+def exchange(value, axis, order):
+    return lax.all_to_all(value, axis, 0, 0, axis_index_groups=[order], tiled=True)
 
 
 def on_device(q_in, k_in, v_in, fir, skip, taps, segments, gain):
@@ -192,7 +201,7 @@
         k_in, v_in, q_in, segments.reshape(1, TB),
         fir, skip.reshape(1, width), taps, gain.reshape(1, width),
     )
-    payload = lax.all_to_all(payload, "ctx", 0, 0, tiled=True)
+    payload = exchange(payload, "ctx", CTX_ORDER)
     mixed = pl.pallas_call(
         conv_kernel,
         out_shape=pltpu.VMEM((NB, CH, TB), BF16),
@@ -200,7 +209,7 @@
         out_specs=VM,
         name="conv",
     )(keep(payload), keep(band), keep(weight))
-    mixed = lax.all_to_all(mixed, "ctx", 0, 0, tiled=True).reshape(width, TB)
+    mixed = exchange(mixed, "ctx", CTX_ORDER)
     part, turned = pl.pallas_call(
         square_kernel,
         out_shape=(pltpu.VMEM((NB, 1, TB), F32), pltpu.VMEM((TB, width), F32)),
@@ -208,7 +217,7 @@
         out_specs=(VM,) * 2,
         name="squares",
     )(keep(mixed), keep(gate), keep(payload), keep(rows))
-    part = lax.all_to_all(part, "grp", 0, 0, tiled=True)
+    part = exchange(part, "grp", GRP_ORDER)
     return pl.pallas_call(
         finish_kernel,
         out_shape=jax.ShapeDtypeStruct((TB, width), BF16),

time: 46.5 us -> 39.5 us (0.85)
  blocking collectives: 42.9 us -> 36 us
    all_to_all x3, blocking collectives: 42.9 us -> 36 us  [exchange(): lax.all_to_all(value, axis, 0, 0, axis_index_groups=[order], tiled=True)]
where the time goes in v7:
time: 39.5 us; the launch traced here: 39.3 us
  blocking collectives  36 us (91%)
  Pallas kernels  3.31 us (8%)
    all_to_all x3, blocking collectives, exchange(): lax.all_to_all(value, axis, 0, 0, axis_index_groups=[order], tiled=True)  36 us
    pallas_call x1, Pallas kernels, on_device(): pl.pallas_call(prepare_kernel, out_shape=(pltpu.VMEM((NB, ROWS, TB), BF16...  1.65 us

profile of v7, /device:TPU:1, one launch (start us, length us, event | category | flops | bytes accessed | tf_op | source)
XLA Modules:
  0.0 39.3 jit_solution(7579306999651143689)
XLA Ops:
  0.0 1.6 %prepare.1 = (bf16[16,48,128]{2,1,0:T(8,128)(2,1)S(1)}, bf16[17,128,128]{2,1,0:T(8,128)(2,1)S(1)}, f32[7,32,128]{2,1,0:T(8,128)S(1)}, f32[512,128]{1,0:T(8,128)S(1)}, f32[8,512]{1,0:T(8,128)S(1)}) custom-call(bf16[128,512]{1,0:T(8,128)(2,1)} %k_ref.1, bf16[128,512]{1,0:T(8,128)(2,1)} %v_ref.1, bf16[128,512]{1,0:T(8,128)(2,1)} %q_ref.1, s32[1,128]{1,0:T(1,128)} %bitcast.5, ...), custom_call_target="tpu_custom_call" | custom-call | tf_op jit(solution)/shard_map/prepare/pallas_call | solution.py:187
  1.7 11.7 %all_to_all.15.x_ref = bf16[16,48,128]{2,1,0:T(8,128)(2,1)S(1)} all-to-all(bf16[16,48,128]{2,1,0:T(8,128)(2,1)S(1)} %get-tuple-element.12), channel_id=1, replica_groups={{160,176,192,208,224,240,0,16,32,48,64,80,96,112,128,144},{161,177,193,..., dimensions={0} | all-to-all | bytes 393216 | tf_op jit(solution)/shard_map/all_to_all | solution.py:182
  13.4 0.7 %conv.1 = bf16[16,32,128]{2,1,0:T(8,128)(2,1)S(1)} custom-call(bf16[16,48,128]{2,1,0:T(8,128)(2,1)S(1)} %all_to_all.15.x_ref, bf16[17,128,128]{2,1,0:T(8,128)(2,1)S(1)} %get-tuple-element.13.band_ref, f32[7,32,128]{2,1,0:T(8,128)S(1)} %get-tuple-element.14.weight_ref), custom_call_target="tpu_custom_call" | custom-call | tf_op jit(solution)/shard_map/conv/pallas_call | solution.py:205
  14.0 9.5 %all_to_all.16.u_ref = bf16[16,32,128]{2,1,0:T(8,128)(2,1)S(1)} all-to-all(bf16[16,32,128]{2,1,0:T(8,128)(2,1)S(1)} %conv.1), channel_id=1, replica_groups={{160,176,192,208,224,240,0,16,32,48,64,80,96,112,128,144},{161,177,193,..., dimensions={0} | all-to-all | bytes 262144 | tf_op jit(solution)/shard_map/all_to_all | solution.py:182
  23.6 0.2 squares.1
  23.8 14.7 %all_to_all.17.part_ref = f32[16,1,128]{2,1,0:T(1,128)S(1)} all-to-all(f32[16,1,128]{2,1,0:T(1,128)S(1)} %get-tuple-element.18), channel_id=1, replica_groups={{9,10,11,12,13,14,15,0,1,2,3,4,5,6,7,8},{25,26,27,28,29,30,31,16,17,18,..., dimensions={0} | all-to-all | bytes 16384 | tf_op jit(solution)/shard_map/all_to_all | solution.py:182
  38.5 0.8 %finish.1 = bf16[128,512]{1,0:T(8,128)(2,1)} custom-call(f32[128,512]{1,0:T(8,128)S(1)} %get-tuple-element.17.x_ref, f32[16,1,128]{2,1,0:T(1,128)S(1)} %all_to_all.17.part_ref), custom_call_target="tpu_custom_call" | custom-call | tf_op jit(solution)/shard_map/finish/pallas_call | solution.py:221

commit v8 on v7

--- a/solution.py
+++ b/solution.py
@@ -36,6 +36,17 @@
     index = lax.axis_index("ctx")
     row_at = lax.broadcasted_iota(jnp.int32, (TB, TB), 0)
     col_at = lax.broadcasted_iota(jnp.int32, (TB, TB), 1)
+    taps = taps_ref[...].astype(F32)
+    pick = lax.broadcasted_iota(jnp.int32, taps.shape, 0) == index // 4
+    row = jnp.sum(jnp.where(pick, taps, 0.0), axis=0, keepdims=True)
+    upper = col_at >= row_at
+    before = jnp.zeros((TB, TB), F32)
+    band_ref[0] = before.astype(BF16)
+    for m in range(NB):
+        piece = jnp.broadcast_to(row[:, m * TB : (m + 1) * TB], (TB, TB))
+        rolled = pltpu.roll(piece, 0, 1, stride=1, stride_axis=0)
+        band_ref[m + 1] = jnp.where(upper, rolled, before).astype(BF16)
+        before = rolled
     same = jnp.where(row_at == col_at, 1.0, 0.0).astype(BF16)
     first = jnp.sum(jnp.where(seg_ref[...] == 0, 1.0, 0.0), axis=1, keepdims=True)
     tail = q_ref[TB - 16 :, :].astype(F32)[14:16]
@@ -69,18 +80,6 @@
     row_ref[0:3] = fir_ref[0]
     row_ref[3:4] = gain_ref[...]
 
-    taps = taps_ref[...].astype(F32)
-    pick = lax.broadcasted_iota(jnp.int32, taps.shape, 0) == index // 4
-    row = jnp.sum(jnp.where(pick, taps, 0.0), axis=0, keepdims=True)
-    upper = col_at >= row_at
-    before = jnp.zeros((TB, TB), F32)
-    band_ref[0] = before.astype(BF16)
-    for m in range(NB):
-        piece = jnp.broadcast_to(row[:, m * TB : (m + 1) * TB], (TB, TB))
-        rolled = pltpu.roll(piece, 0, 1, stride=1, stride_axis=0)
-        band_ref[m + 1] = jnp.where(upper, rolled, before).astype(BF16)
-        before = rolled
-
 
 def conv_kernel(x_ref, band_ref, weight_ref, out_ref):
     lane = lax.broadcasted_iota(jnp.int32, (CH, TB), 1)
@@ -104,7 +103,8 @@
     product, second, masks, after = [], [], [], []
     for a in range(NB):
         value = x_ref[PLACE[a], 0:CH, :].astype(F32)
-        first = jnp.broadcast_to(value[:, 0:1], (CH, TB))
+        first = jnp.broadcast_to(value[0:8, 0:1], (8, TB))
+        first = jnp.concatenate([first] * 4, axis=0)
         mask = lane.astype(F32) >= first
         if a % 2 == 0:
             after.append(jnp.concatenate([first, first], axis=1) == 0.0)

time: 39.5 us -> 39.4 us (level)
  no operation moved by 1% of the time
where the time goes in v8:
time: 39.4 us; the launch traced here: 39.2 us
  blocking collectives  36 us (91%)
  Pallas kernels  3.22 us (8%)
    all_to_all x3, blocking collectives, exchange(): lax.all_to_all(value, axis, 0, 0, axis_index_groups=[order], tiled=True)  36 us
    pallas_call x1, Pallas kernels, on_device(): pl.pallas_call(prepare_kernel, out_shape=(pltpu.VMEM((NB, ROWS, TB), BF16...  1.58 us

profile of v8, /device:TPU:1, one launch (start us, length us, event | category | flops | bytes accessed | tf_op | source)
XLA Modules:
  0.0 39.2 jit_solution(1619929527633109842)
XLA Ops:
  0.0 1.6 %prepare.1 = (bf16[16,48,128]{2,1,0:T(8,128)(2,1)S(1)}, bf16[17,128,128]{2,1,0:T(8,128)(2,1)S(1)}, f32[7,32,128]{2,1,0:T(8,128)S(1)}, f32[512,128]{1,0:T(8,128)S(1)}, f32[8,512]{1,0:T(8,128)S(1)}) custom-call(bf16[128,512]{1,0:T(8,128)(2,1)} %k_ref.1, bf16[128,512]{1,0:T(8,128)(2,1)} %v_ref.1, bf16[128,512]{1,0:T(8,128)(2,1)} %q_ref.1, s32[1,128]{1,0:T(1,128)} %bitcast.5, ...), custom_call_target="tpu_custom_call" | custom-call | tf_op jit(solution)/shard_map/prepare/pallas_call | solution.py:187
  1.6 11.7 %all_to_all.15.x_ref = bf16[16,48,128]{2,1,0:T(8,128)(2,1)S(1)} all-to-all(bf16[16,48,128]{2,1,0:T(8,128)(2,1)S(1)} %get-tuple-element.12), channel_id=1, replica_groups={{160,176,192,208,224,240,0,16,32,48,64,80,96,112,128,144},{161,177,193,..., dimensions={0} | all-to-all | bytes 393216 | tf_op jit(solution)/shard_map/all_to_all | solution.py:182
  13.3 0.6 %conv.1 = bf16[16,32,128]{2,1,0:T(8,128)(2,1)S(1)} custom-call(bf16[16,48,128]{2,1,0:T(8,128)(2,1)S(1)} %all_to_all.15.x_ref, bf16[17,128,128]{2,1,0:T(8,128)(2,1)S(1)} %get-tuple-element.13.band_ref, f32[7,32,128]{2,1,0:T(8,128)S(1)} %get-tuple-element.14.weight_ref), custom_call_target="tpu_custom_call" | custom-call | tf_op jit(solution)/shard_map/conv/pallas_call | solution.py:205
  13.9 9.5 %all_to_all.16.u_ref = bf16[16,32,128]{2,1,0:T(8,128)(2,1)S(1)} all-to-all(bf16[16,32,128]{2,1,0:T(8,128)(2,1)S(1)} %conv.1), channel_id=1, replica_groups={{160,176,192,208,224,240,0,16,32,48,64,80,96,112,128,144},{161,177,193,..., dimensions={0} | all-to-all | bytes 262144 | tf_op jit(solution)/shard_map/all_to_all | solution.py:182
  23.5 0.2 squares.1
  23.7 14.7 %all_to_all.17.part_ref = f32[16,1,128]{2,1,0:T(1,128)S(1)} all-to-all(f32[16,1,128]{2,1,0:T(1,128)S(1)} %get-tuple-element.18), channel_id=1, replica_groups={{9,10,11,12,13,14,15,0,1,2,3,4,5,6,7,8},{25,26,27,28,29,30,31,16,17,18,..., dimensions={0} | all-to-all | bytes 16384 | tf_op jit(solution)/shard_map/all_to_all | solution.py:182
  38.4 0.8 %finish.1 = bf16[128,512]{1,0:T(8,128)(2,1)} custom-call(f32[128,512]{1,0:T(8,128)S(1)} %get-tuple-element.17.x_ref, f32[16,1,128]{2,1,0:T(1,128)S(1)} %all_to_all.17.part_ref), custom_call_target="tpu_custom_call" | custom-call | tf_op jit(solution)/shard_map/finish/pallas_call | solution.py:221

commit v9 on v8

--- a/solution.py
+++ b/solution.py
@@ -20,22 +20,26 @@
 BF16 = jnp.bfloat16
 
 
-def fir_filter(ref, fir_ref, which, lanes, row_at=None):
+def fir_filter(ref, taps, lanes, row_at=None):
     value = ref[:, lanes].astype(F32)
     one, two = pltpu.roll(value, 1, 0), pltpu.roll(value, 2, 0)
     if row_at is not None:
         one, two = jnp.where(row_at == 0, 0.0, one), jnp.where(row_at <= 1, 0.0, two)
-    taps = [fir_ref[which, n : n + 1, lanes] for n in range(3)]
     return taps[0] * value + taps[1] * one + taps[2] * two
 
 
-def prepare_kernel(
-    k_ref, v_ref, q_ref, seg_ref, fir_ref, skip_ref, taps_ref, gain_ref,
-    out_ref, band_ref, weight_ref, gate_ref, row_ref, coef_ref,
-):
+def prepare_kernel(*refs):
+    sources, outs, coef_ref, sems = refs[:8], refs[8:13], refs[20], refs[21]
+    buffers = refs[13:16] + refs[12:13] + refs[16:20]
+    taps_ref, k_ref, v_ref, q_ref, fir_ref, skip_ref, gain_ref, seg_ref = buffers
+    out_ref, band_ref, weight_ref, row_ref = outs[:4]
+    copies = [pltpu.make_async_copy(src, dst, sems.at[n]) for n, (src, dst) in enumerate(zip(sources, buffers))]
+    for copy in copies:
+        copy.start()
     index = lax.axis_index("ctx")
     row_at = lax.broadcasted_iota(jnp.int32, (TB, TB), 0)
     col_at = lax.broadcasted_iota(jnp.int32, (TB, TB), 1)
+    copies[0].wait()
     taps = taps_ref[...].astype(F32)
     pick = lax.broadcasted_iota(jnp.int32, taps.shape, 0) == index // 4
     row = jnp.sum(jnp.where(pick, taps, 0.0), axis=0, keepdims=True)
@@ -47,6 +51,8 @@
         rolled = pltpu.roll(piece, 0, 1, stride=1, stride_axis=0)
         band_ref[m + 1] = jnp.where(upper, rolled, before).astype(BF16)
         before = rolled
+    for copy in copies[1:]:
+        copy.wait()
     same = jnp.where(row_at == col_at, 1.0, 0.0).astype(BF16)
     first = jnp.sum(jnp.where(seg_ref[...] == 0, 1.0, 0.0), axis=1, keepdims=True)
     tail = q_ref[TB - 16 :, :].astype(F32)[14:16]
@@ -56,12 +62,12 @@
     edges = jnp.concatenate([heads[0], tails[0], heads[1], tails[1]], axis=0)
     for n in range(4):
         lanes = slice(n * TB, (n + 1) * TB)
-        value = fir_filter(k_ref, fir_ref, 1, lanes) * fir_filter(v_ref, fir_ref, 2, lanes)
+        k_taps, v_taps = ([fir_ref[a, m : m + 1, lanes] for m in range(3)] for a in (1, 2))
+        value = fir_filter(k_ref, k_taps, lanes) * fir_filter(v_ref, v_taps, lanes)
         value = lax.dot_general(
             same, value.astype(BF16), (((1,), (1,)), ((), ())), preferred_element_type=F32
         )
         value = jnp.where(col_at == 0, first, value).astype(BF16)
-        gate_ref[lanes, :] = fir_filter(q_ref, fir_ref, 0, lanes, row_at).T
         for m in range(4):
             here = jnp.where(index == 4 * n + m - 1, tail, 0.0)
             edge = pltpu.roll(edges[:, lanes], (TB - m * CH) % TB, 1) if m else edges[:, lanes]
@@ -81,7 +87,11 @@
     row_ref[3:4] = gain_ref[...]
 
 
-def conv_kernel(x_ref, band_ref, weight_ref, out_ref):
+def conv_kernel(x_ref, band_ref, weight_ref, q_ref, row_ref, out_ref, gate_ref):
+    row_at = lax.broadcasted_iota(jnp.int32, (TB, TB), 0)
+    for n in range(4):
+        lanes = slice(n * TB, (n + 1) * TB)
+        gate_ref[lanes, :] = fir_filter(q_ref, [row_ref[m : m + 1, lanes] for m in range(3)], lanes, row_at).T
     lane = lax.broadcasted_iota(jnp.int32, (CH, TB), 1)
     edges = jnp.concatenate([x_ref[PLACE[a], HALO:, :].astype(F32)[8:16] for a in range(NB)], axis=0).T[0:CH]
 
@@ -184,31 +194,33 @@
 
 def on_device(q_in, k_in, v_in, fir, skip, taps, segments, gain):
     width = q_in.shape[1]
-    payload, band, weight, gate, rows = pl.pallas_call(
+    sources = (
+        taps, k_in, v_in, q_in, fir, skip.reshape(1, width), gain.reshape(1, width),
+        segments.reshape(1, TB),
+    )
+    payload, band, weight, rows, query = pl.pallas_call(
         prepare_kernel,
         out_shape=(
             pltpu.VMEM((NB, ROWS, TB), BF16),
             pltpu.VMEM((NB + 1, TB, TB), BF16),
             pltpu.VMEM((7, CH, TB), F32),
-            pltpu.VMEM((width, TB), F32),
             pltpu.VMEM((8, width), F32),
+            pltpu.VMEM((TB, width), BF16),
         ),
-        in_specs=[VM] * 8,
+        in_specs=[pl.BlockSpec(memory_space=pl.ANY)] * 8,
         out_specs=(VM,) * 5,
-        scratch_shapes=[pltpu.VMEM((GW, GW), F32)],
+        scratch_shapes=[pltpu.VMEM(value.shape, value.dtype) for value in sources if value is not q_in]
+        + [pltpu.VMEM((GW, GW), F32), pltpu.SemaphoreType.DMA((8,))],
         name="prepare",
-    )(
-        k_in, v_in, q_in, segments.reshape(1, TB),
-        fir, skip.reshape(1, width), taps, gain.reshape(1, width),
-    )
+    )(*sources)
     payload = exchange(payload, "ctx", CTX_ORDER)
-    mixed = pl.pallas_call(
+    mixed, gate = pl.pallas_call(
         conv_kernel,
-        out_shape=pltpu.VMEM((NB, CH, TB), BF16),
-        in_specs=[VM] * 3,
-        out_specs=VM,
+        out_shape=(pltpu.VMEM((NB, CH, TB), BF16), pltpu.VMEM((width, TB), F32)),
+        in_specs=[VM] * 5,
+        out_specs=(VM,) * 2,
         name="conv",
-    )(keep(payload), keep(band), keep(weight))
+    )(keep(payload), keep(band), keep(weight), keep(query), keep(rows))
     mixed = exchange(mixed, "ctx", CTX_ORDER)
     part, turned = pl.pallas_call(
         square_kernel,

time: 39.4 us -> 39.4 us (level)
  no operation moved by 1% of the time
where the time goes in v9:
time: 39.4 us; the launch traced here: 39.1 us
  blocking collectives  36 us (91%)
  Pallas kernels  3.12 us (8%)
    all_to_all x3, blocking collectives, exchange(): lax.all_to_all(value, axis, 0, 0, axis_index_groups=[order], tiled=True)  36 us
    pallas_call x1, Pallas kernels, on_device(): pl.pallas_call(prepare_kernel, out_shape=(pltpu.VMEM((NB, ROWS, TB), BF16...  1.48 us

profile of v9, /device:TPU:1, one launch (start us, length us, event | category | flops | bytes accessed | tf_op | source)
XLA Modules:
  0.0 39.1 jit_solution(14537573297490320401)
XLA Ops:
  0.0 1.5 %prepare.1 = (bf16[16,48,128]{2,1,0:T(8,128)(2,1)S(1)}, bf16[17,128,128]{2,1,0:T(8,128)(2,1)S(1)}, f32[7,32,128]{2,1,0:T(8,128)S(1)}, f32[8,512]{1,0:T(8,128)S(1)}, bf16[128,512]{1,0:T(8,128)(2,1)S(1)}) custom-call(bf16[4,2048]{1,0:T(4,128)(2,1)} %refs_0_.1, bf16[128,512]{1,0:T(8,128)(2,1)} %refs_1_.1, bf16[128,512]{1,0:T(8,128)(2,1)} %refs_2_.1, ...), custom_call_target="tpu_custom_call" | custom-call | tf_op jit(solution)/shard_map/prepare/pallas_call | solution.py:201
  1.5 11.7 %all_to_all.15.x_ref = bf16[16,48,128]{2,1,0:T(8,128)(2,1)S(1)} all-to-all(bf16[16,48,128]{2,1,0:T(8,128)(2,1)S(1)} %get-tuple-element.14), channel_id=1, replica_groups={{160,176,192,208,224,240,0,16,32,48,64,80,96,112,128,144},{161,177,193,..., dimensions={0} | all-to-all | bytes 393216 | tf_op jit(solution)/shard_map/all_to_all | solution.py:192
  13.2 0.6 %conv.1 = (bf16[16,32,128]{2,1,0:T(8,128)(2,1)S(1)}, f32[512,128]{1,0:T(8,128)S(1)}) custom-call(bf16[16,48,128]{2,1,0:T(8,128)(2,1)S(1)} %all_to_all.15.x_ref, bf16[17,128,128]{2,1,0:T(8,128)(2,1)S(1)} %get-tuple-element.15.band_ref, f32[7,32,128]{2,1,0:T(8,128)S(1)} %get-tuple-element.16.weight_ref, bf16[128,512]{1,0:T(8,128)(2,1)S(1)} %get-tuple-element.17.q_ref, ...), custom_call_target="tpu_custom_call" | custom-call | tf_op jit(solution)/shard_map/conv/pallas_call | solution.py:217
  13.8 9.5 %all_to_all.16.u_ref = bf16[16,32,128]{2,1,0:T(8,128)(2,1)S(1)} all-to-all(bf16[16,32,128]{2,1,0:T(8,128)(2,1)S(1)} %get-tuple-element.19), channel_id=1, replica_groups={{160,176,192,208,224,240,0,16,32,48,64,80,96,112,128,144},{161,177,193,..., dimensions={0} | all-to-all | bytes 262144 | tf_op jit(solution)/shard_map/all_to_all | solution.py:192
  23.4 0.2 squares.1
  23.6 14.7 %all_to_all.17.part_ref = f32[16,1,128]{2,1,0:T(1,128)S(1)} all-to-all(f32[16,1,128]{2,1,0:T(1,128)S(1)} %get-tuple-element.22), channel_id=1, replica_groups={{9,10,11,12,13,14,15,0,1,2,3,4,5,6,7,8},{25,26,27,28,29,30,31,16,17,18,..., dimensions={0} | all-to-all | bytes 16384 | tf_op jit(solution)/shard_map/all_to_all | solution.py:192
  38.3 0.8 %finish.1 = bf16[128,512]{1,0:T(8,128)(2,1)} custom-call(f32[128,512]{1,0:T(8,128)S(1)} %get-tuple-element.21.x_ref, f32[16,1,128]{2,1,0:T(1,128)S(1)} %all_to_all.17.part_ref), custom_call_target="tpu_custom_call" | custom-call | tf_op jit(solution)/shard_map/finish/pallas_call | solution.py:233
